TPU v7x, 256 devices: a whole 4x4x8 slice. The times are simulated.
256 devices in a mesh: node: 32 (over z_lo, y, x), col: 8 (over z_hi, core).
Axes of the slice: x: 4, y: 4, z: 8 (z_hi: 4, z_lo: 2; z = z_hi * 2 + z_lo), core: 2. Of those that a mesh axis runs over, the one named last changes fastest.
Arguments:
- coefficients: bfloat16 [128, 256, 8192], P('node', None, 'col'), may hold values from -6 to 6
- transfer: bfloat16 [3, 128, 4, 256, 256], P(None, 'node', None, 'col'), may hold values from -0.1875 to 0.1875
Outputs:
- result: bfloat16 [128, 256, 8192], P('node', None, 'col')
All inputs are finite; a program needn't handle non-finite values.
Results may differ from a plain program's by a relative error of at most 0.0058.
Values may be sent and summed in bfloat16 or wider, within the bound.
No kernel may reach another device: no remote copies, remote signals or barrier semaphores. Data moves between devices by JAX's collectives and lax.ppermute only.
A program may use at most 64 MiB of HBM per device.

v0:
```python
import jax
import jax.numpy as jnp
from jax import lax
from jax.sharding import PartitionSpec as P


def from_partner(array, axis, apart):
    return lax.ppermute(array, axis, [(i, i ^ 1 << apart) for i in range(lax.axis_size(axis))])


def local(coefficients, transfer):
    position = lax.axis_index("node")
    current = coefficients
    for level_index in range(3):
        weights_now = transfer[level_index]
        if level_index == 0:
            operand = current[:, None]
            form = "lers,emsc->lrc"
        else:
            bit_base = 2 * (level_index - 1)
            own_digit = position // 4 ** (level_index - 1) % 4
            partner_one = from_partner(current, "node", bit_base)
            partner_two, partner_three = from_partner((current, partner_one), "node", bit_base + 1)
            operand = jnp.stack([current, partner_one, partner_two, partner_three])
            order_idx = jnp.bitwise_xor(jnp.arange(4, dtype=jnp.int32), own_digit)
            weights_now = jnp.take(weights_now, order_idx, axis=1)
            form = "lers,elsc->lrc"
        mixed = jnp.einsum(
            form,
            lax.all_gather(weights_now, "col", axis=2, tiled=True),
            operand,
            preferred_element_type=jnp.float32,
        )
        current = mixed.astype(jnp.bfloat16)
    return current


def solution(mesh):
    return jax.shard_map(
        local,
        mesh=mesh,
        in_specs=(P("node", None, "col"), P(None, "node", None, "col", None)),
        out_specs=P("node", None, "col"),
        check_vma=False,
    )
```

profile of v0, /device:TPU:62, one launch (start us, length us, event | category | flops | bytes accessed | tf_op | source)
XLA Modules:
  0.0 346.5 jit_solution(3586287271319052028)
XLA Ops:
  6.5 2.0 fusion.12
  8.6 0.0 all-gather.9.cloned.1.call-update
  8.6 0.0 all-gather.7.cloned.1.call-start
  8.7 38.3 %all-gather.9.cloned.1.call-done = bf16[1,4,4,256,256]{4,3,2,1,0:T(8,128)(2,1)} async-done(((bf16[1,4,4,32,256]{4,3,2,1,0:T(8,128)(2,1)}), bf16[1,4,4,256,256]{4,3,2,1,0:T(8,128)(2,1)}) %all-gather.9.cloned.1.call-update) | async-done | bytes 2097168 | tf_op jit(solution)/shard_map/all_gather | solution.py:30
  46.9 5.2 %bitcast_convert_fusion.2 = bf16[4,256,1024]{2,1,0:T(8,128)(2,1)} fusion(bf16[4,256,1024]{2,1,0:T(8,128)(2,1)S(1)} %copy-done, bf16[1,4,4,256,256]{4,3,2,1,0:T(8,128)(2,1)} %all-gather.9.cloned.1.call-done), kind=kOutput, calls=%fused_computation.10 | convolution fusion | flops 2148532224 | bytes 6291456 | tf_op jit(solution)/shard_map/lers,emsc->lrc/dot_general | solution.py:28
  52.1 0.8 collective-permute-start
  53.0 0.6 gather_fusion.1
  53.6 0.8 fusion.10
  54.4 0.0 all-gather.5.cloned.1.call-start
  54.4 1.2 collective-permute-start.1
  55.7 45.2 %collective-permute-done = bf16[4,256,1024]{2,1,0:T(8,128)(2,1)} collective-permute-done((bf16[4,256,1024]{2,1,0:T(8,128)(2,1)}, bf16[4,256,1024]{2,1,0:T(8,128)(2,1)}, u32[]{:S(2)}, u32[]{:S(2)}) %collective-permute-start) | collective-permute-done | bytes 2097184 | tf_op jit(solution)/shard_map/ppermute | solution.py:8
  100.9 1.5 collective-permute-start.2
  102.4 43.5 %collective-permute-done.1 = bf16[4,256,1024]{2,1,0:T(8,128)(2,1)} collective-permute-done((bf16[4,256,1024]{2,1,0:T(8,128)(2,1)}, bf16[4,256,1024]{2,1,0:T(8,128)(2,1)}, u32[]{:S(2)}, u32[]{:S(2)}) %collective-permute-start.1) | collective-permute-done | bytes 2097184 | tf_op jit(solution)/shard_map/ppermute | solution.py:8
  145.8 44.3 %collective-permute-done.2 = bf16[4,256,1024]{2,1,0:T(8,128)(2,1)} collective-permute-done((bf16[4,256,1024]{2,1,0:T(8,128)(2,1)}, bf16[4,256,1024]{2,1,0:T(8,128)(2,1)}, u32[]{:S(2)}, u32[]{:S(2)}) %collective-permute-start.2) | collective-permute-done | bytes 2097184 | tf_op jit(solution)/shard_map/ppermute | solution.py:8
  190.1 6.4 %bitcast_convert_fusion.1 = bf16[4,256,1024]{2,1,0:T(8,128)(2,1)} fusion(bf16[4,4,256,256]{3,2,1,0:T(8,128)(2,1)} %all-gather.7.cloned.1.call-done, bf16[1,4,256,1024]{3,2,1,0:T(8,128)(2,1)} %bitcast.11, bf16[1,4,256,1024]{3,2,1,0:T(8,128)(2,1)} %bitcast.10, bf16[1,4,256,1024]{3,2,1,0:T(8,128)(2,1)} %bitcast.9, bf16[1,4,256,1024]{3,2,1,0:T(8,128)(2,1)} %bitcast.8), kind=kOutput, calls=%fused_computation.9 | convolution fusion | flops 2161115136 | bytes 12582912 | tf_op jit(solution)/shard_map/lers,elsc->lrc/dot_general | solution.py:28
  196.5 0.8 collective-permute-start.3
  197.4 0.6 gather_fusion
  197.9 0.8 fusion.11
  198.8 1.2 collective-permute-start.4
  200.0 45.4 %collective-permute-done.3 = bf16[4,256,1024]{2,1,0:T(8,128)(2,1)} collective-permute-done((bf16[4,256,1024]{2,1,0:T(8,128)(2,1)}, bf16[4,256,1024]{2,1,0:T(8,128)(2,1)}, u32[]{:S(2)}, u32[]{:S(2)}) %collective-permute-start.3) | collective-permute-done | bytes 2097184 | tf_op jit(solution)/shard_map/ppermute | solution.py:8
  245.4 1.4 collective-permute-start.5
  246.8 43.5 %collective-permute-done.4 = bf16[4,256,1024]{2,1,0:T(8,128)(2,1)} collective-permute-done((bf16[4,256,1024]{2,1,0:T(8,128)(2,1)}, bf16[4,256,1024]{2,1,0:T(8,128)(2,1)}, u32[]{:S(2)}, u32[]{:S(2)}) %collective-permute-start.4) | collective-permute-done | bytes 2097184 | tf_op jit(solution)/shard_map/ppermute | solution.py:8
  290.3 43.4 %collective-permute-done.5 = bf16[4,256,1024]{2,1,0:T(8,128)(2,1)} collective-permute-done((bf16[4,256,1024]{2,1,0:T(8,128)(2,1)}, bf16[4,256,1024]{2,1,0:T(8,128)(2,1)}, u32[]{:S(2)}, u32[]{:S(2)}) %collective-permute-start.5) | collective-permute-done | bytes 2097184 | tf_op jit(solution)/shard_map/ppermute | solution.py:8
  333.7 6.3 %bitcast_convert_fusion = bf16[4,256,1024]{2,1,0:T(8,128)(2,1)} fusion(bf16[4,4,256,256]{3,2,1,0:T(8,128)(2,1)} %all-gather.5.cloned.1.call-done, bf16[1,4,256,1024]{3,2,1,0:T(8,128)(2,1)} %bitcast.17, bf16[1,4,256,1024]{3,2,1,0:T(8,128)(2,1)} %bitcast.16, bf16[1,4,256,1024]{3,2,1,0:T(8,128)(2,1)} %bitcast.15, bf16[1,4,256,1024]{3,2,1,0:T(8,128)(2,1)} %bitcast.14), kind=kOutput, calls=%fused_computation.8 | convolution fusion | flops 2161115136 | bytes 12582912 | tf_op jit(solution)/shard_map/lers,elsc->lrc/dot_general | solution.py:28
  (13 shorter events, 0.1 us)
Async XLA Ops:
  6.5 40.4 %copy-start = (bf16[4,256,1024]{2,1,0:T(8,128)(2,1)S(1)}, bf16[4,256,1024]{2,1,0:T(8,128)(2,1)}, u32[]{:S(2)}) copy-start(bf16[4,256,1024]{2,1,0:T(8,128)(2,1)} %param.4) | copy-start | bytes 6291460
  6.5 40.4 %all-gather.9.cloned.1.call-start = ((), (), s32[]{:S(2)}) async-start(), calls=%async_computation.2 | async-start | bytes 2359296 | tf_op jit(solution)/shard_map/all_gather | solution.py:30
  8.6 93.8 %all-gather.7.cloned.1.call-start = ((), (), s32[]{:S(2)}) async-start(), calls=%async_computation.1 | async-start | bytes 2359296 | tf_op jit(solution)/shard_map/all_gather | solution.py:30
  52.1 48.8 %collective-permute-start = (bf16[4,256,1024]{2,1,0:T(8,128)(2,1)}, bf16[4,256,1024]{2,1,0:T(8,128)(2,1)}, u32[]{:S(2)}, u32[]{:S(2)}) collective-permute-start(bf16[4,256,1024]{2,1,0:T(8,128)(2,1)} %bitcast_convert_fusion.2), channel_id=1, source_target_pairs={{0,8},{8,0},{16,24},{24,16},{32,40},{40,32},{48,56},{56,48},{64,72... | collective-permute-start | bytes 6291464 | tf_op jit(solution)/shard_map/ppermute | solution.py:8
  54.4 192.4 %all-gather.5.cloned.1.call-start = ((), (), s32[]{:S(2)}) async-start(), calls=%async_computation | async-start | bytes 2359296 | tf_op jit(solution)/shard_map/all_gather | solution.py:30
  54.4 91.4 %collective-permute-start.1 = (bf16[4,256,1024]{2,1,0:T(8,128)(2,1)}, bf16[4,256,1024]{2,1,0:T(8,128)(2,1)}, u32[]{:S(2)}, u32[]{:S(2)}) collective-permute-start(bf16[4,256,1024]{2,1,0:T(8,128)(2,1)} %bitcast_convert_fusion.2), channel_id=1, source_target_pairs={{0,16},{8,24},{16,0},{24,8},{32,48},{40,56},{48,32},{56,40},{64,80... | collective-permute-start | bytes 6291464 | tf_op jit(solution)/shard_map/ppermute | solution.py:8
  100.9 89.2 %collective-permute-start.2 = (bf16[4,256,1024]{2,1,0:T(8,128)(2,1)}, bf16[4,256,1024]{2,1,0:T(8,128)(2,1)}, u32[]{:S(2)}, u32[]{:S(2)}) collective-permute-start(bf16[4,256,1024]{2,1,0:T(8,128)(2,1)} %collective-permute-done), channel_id=1, source_target_pairs={{0,16},{8,24},{16,0},{24,8},{32,48},{40,56},{48,32},{56,40},{64,80... | collective-permute-start | bytes 6291464 | tf_op jit(solution)/shard_map/ppermute | solution.py:8
  196.5 48.9 %collective-permute-start.3 = (bf16[4,256,1024]{2,1,0:T(8,128)(2,1)}, bf16[4,256,1024]{2,1,0:T(8,128)(2,1)}, u32[]{:S(2)}, u32[]{:S(2)}) collective-permute-start(bf16[4,256,1024]{2,1,0:T(8,128)(2,1)} %bitcast_convert_fusion.1), channel_id=1, source_target_pairs={{0,32},{8,40},{16,48},{24,56},{32,0},{40,8},{48,16},{56,24},{64,96... | collective-permute-start | bytes 6291464 | tf_op jit(solution)/shard_map/ppermute | solution.py:8
  198.8 91.5 %collective-permute-start.4 = (bf16[4,256,1024]{2,1,0:T(8,128)(2,1)}, bf16[4,256,1024]{2,1,0:T(8,128)(2,1)}, u32[]{:S(2)}, u32[]{:S(2)}) collective-permute-start(bf16[4,256,1024]{2,1,0:T(8,128)(2,1)} %bitcast_convert_fusion.1), channel_id=1, source_target_pairs={{0,64},{8,72},{16,80},{24,88},{32,96},{40,104},{48,112},{56,120},{... | collective-permute-start | bytes 6291464 | tf_op jit(solution)/shard_map/ppermute | solution.py:8
  245.4 88.3 %collective-permute-start.5 = (bf16[4,256,1024]{2,1,0:T(8,128)(2,1)}, bf16[4,256,1024]{2,1,0:T(8,128)(2,1)}, u32[]{:S(2)}, u32[]{:S(2)}) collective-permute-start(bf16[4,256,1024]{2,1,0:T(8,128)(2,1)} %collective-permute-done.3), channel_id=1, source_target_pairs={{0,64},{8,72},{16,80},{24,88},{32,96},{40,104},{48,112},{56,120},{... | collective-permute-start | bytes 6291464 | tf_op jit(solution)/shard_map/ppermute | solution.py:8
Sparse Core Ops, SparseCore 0:
  9.2 37.6 all-gather.8
  54.5 34.4 all-gather.6
  198.9 34.4 all-gather.4
where the time goes:
time: 352 us; the launch traced here: 346 us
  waiting for transfers between devices  303 us (86%)
  matrix products  17.9 us (5%)
  between operations  13.2 us (4%)
  starting transfers between devices  7.13 us (2%)
    ppermute x6, waiting for transfers between devices, from_partner(): lax.ppermute(array, axis, [(i, i ^ 1 << apart) for i in range(lax.axis_si...  265 us
    all_gather x3, waiting for transfers between devices, local(): lax.all_gather(weights_now, 'col', axis=2, tiled=True)  38.3 us
    dot_general x3, matrix products, local(): jnp.einsum(form, lax.all_gather(weights_now, 'col', axis=2, tiled=True),...  17.9 us
    ppermute x6, starting transfers between devices, from_partner(): lax.ppermute(array, axis, [(i, i ^ 1 << apart) for i in range(lax.axis_si...  7.04 us
  transfers between devices with their start and end apart: 9, of which 7 were waited for; matrix products, arithmetic and copies ran while one was open for 1% of the time, Pallas kernels for 0%

commit v1 on v0

v1 whole, which is shorter than its diff:
```python
import functools

import jax
import jax.numpy as jnp
from jax import lax
from jax.experimental import pallas as pl
from jax.experimental.pallas import tpu as pltpu
from jax.sharding import Mesh, PartitionSpec as P

CHUNKS = 2
DIGITS = range(4)


def level_kernel(parent_first, order, own_ref, other_ref, *refs):
    children, outs, weights = refs[:-5], refs[-5:-1], refs[-1]
    core = order[0]
    for half, ref in ((core, own_ref), (1 - core, other_ref)):
        for zh in DIGITS:
            rows = pl.ds(pl.multiple_of(64 * zh + 32 * half, 32), 32)
            for s in DIGITS:
                for p in DIGITS:
                    parent, child = order[1 + s], order[5 + p]
                    piece = ref[parent, zh, child] if parent_first else ref[zh, parent, child]
                    weights[s, p, rows, :] = piece
    blocks = [children[0].at[p] for p in DIGITS] if len(children) == 1 else children
    for s in DIGITS:
        total = sum(
            jnp.dot(weights[s, p], blocks[p][...], preferred_element_type=jnp.float32)
            for p in DIGITS
        )
        outs[s][...] = total.astype(outs[s].dtype)


def level(order, own, other, children, parent_first, chunk):
    whole = lambda a: pl.BlockSpec(a.shape, lambda i, o: (0,) * a.ndim)
    if isinstance(children, (list, tuple)):
        width = children[0].shape[1]
        specs, operands = [whole(a) for a in children], list(children)
    else:
        width = children.shape[2] // CHUNKS
        specs = [pl.BlockSpec((4, 256, width), lambda i, o: (0, 0, chunk))]
        operands = [children]
    return pl.pallas_call(
        functools.partial(level_kernel, parent_first),
        grid_spec=pltpu.PrefetchScalarGridSpec(
            num_scalar_prefetch=1,
            grid=(1,),
            in_specs=[whole(own), whole(other)] + specs,
            out_specs=[pl.BlockSpec((256, width), lambda i, o: (0, 0))] * 4,
            scratch_shapes=[pltpu.VMEM((4, 4, 256, 256), jnp.bfloat16)],
        ),
        out_shape=[jax.ShapeDtypeStruct((256, width), jnp.bfloat16)] * 4,
        cost_estimate=pl.CostEstimate(
            flops=2 * 16 * 256 * 256 * width,
            bytes_accessed=2 * (16 * 256 * 256 + 8 * 256 * width),
            transcendentals=0,
        ),
        compiler_params=pltpu.CompilerParams(vmem_limit_bytes=40 * 2**20),
    )(order, own, other, *operands)


def place_kernel(chunk, width, order, *refs):
    blocks, out, sems = refs[:4], refs[-2], refs[-1]
    copies = [
        pltpu.make_async_copy(
            blocks[s], out.at[order[s], :, pl.ds(chunk * width, width)], sems.at[s]
        )
        for s in DIGITS
    ]
    for copy in copies:
        copy.start()
    for copy in copies:
        copy.wait()


def place(order, blocks, chunk, into):
    width = blocks[0].shape[1]
    extra = [] if into is None else [into]
    anywhere = pl.BlockSpec(memory_space=pl.ANY)
    return pl.pallas_call(
        functools.partial(place_kernel, chunk, width),
        grid_spec=pltpu.PrefetchScalarGridSpec(
            num_scalar_prefetch=1,
            grid=(1,),
            in_specs=[anywhere] * (4 + len(extra)),
            out_specs=anywhere,
            scratch_shapes=[pltpu.SemaphoreType.DMA((4,))],
        ),
        out_shape=jax.ShapeDtypeStruct((4, 256, CHUNKS * width), jnp.bfloat16),
        input_output_aliases={} if into is None else {5: 0},
    )(order, *blocks, *extra)


def shift(array, axis, by):
    size = lax.axis_size(axis)
    return lax.ppermute(array, axis, [(i, (i + by) % size) for i in range(size)])


def swap(array):
    return shift(array, "core", 1)


def gather_weights(shard, axis):
    if axis is None:
        spread = jnp.broadcast_to(shard[None], (4,) + shard.shape)
        got = lax.all_to_all(spread, "zh", 0, 0, tiled=True)
    else:
        spread = jnp.broadcast_to(shard[:, None], (4, 4) + shard.shape[1:])
        got = lax.all_to_all(
            spread.reshape((16,) + shard.shape[1:]), (axis, "zh"), 0, 0, tiled=True
        ).reshape(spread.shape)
    return got, swap(got)


def exchange(blocks, axis):
    return [blocks[0]] + [shift(blocks[s], axis, s) for s in (1, 2, 3)]


def turn(blocks):
    pairs = lambda s: [(4 * b + a, 4 * a + (a + b + s) % 4) for b in DIGITS for a in DIGITS]
    return [lax.ppermute(blocks[s], ("y", "x"), pairs(s)) for s in DIGITS]


def local(coefficients, transfer):
    a, b, core = lax.axis_index("x"), lax.axis_index("y"), lax.axis_index("core")
    steps = jnp.arange(4, dtype=jnp.int32)

    def order(parents, children):
        return jnp.concatenate([core[None], parents % 4, children % 4]).astype(jnp.int32)

    order0 = order(a + steps, steps)
    order1 = order(a + b + steps, a - steps + 4)
    order2 = order(b + steps, a - b - steps + 8)
    orderp = ((b - steps + 4) % 4).astype(jnp.int32)

    w0 = gather_weights(transfer[0], None)
    w1 = gather_weights(transfer[1], "x")
    w2 = gather_weights(transfer[2], "y")
    states = [exchange(level(order0, *w0, coefficients, False, c), "x") for c in range(CHUNKS)]
    states = [turn(level(order1, *w1, s, True, 0)) for s in states]
    states = [exchange(level(order2, *w2, s, True, 0), "y") for s in states]
    result = None
    for c in range(CHUNKS):
        result = place(orderp, states[c], c, result)
    return result


def solution(mesh):
    fine = Mesh(mesh.devices.reshape(2, 4, 4, 4, 2), ("zl", "y", "x", "zh", "core"))
    node, col = ("zl", "y", "x"), ("zh", "core")
    return jax.shard_map(
        local,
        mesh=fine,
        in_specs=(P(node, None, col), P(None, node, None, col, None)),
        out_specs=P(node, None, col),
        check_vma=False,
    )
```

time: 352 us -> 275 us (0.78)
  the two profiles are of different devices: /device:TPU:62 before, /device:TPU:24 now
where the time goes in v1:
time: 275 us
  Pallas kernels  88.6 us (32%)
  blocking collectives  70.4 us (26%)
  starting transfers between devices  62.6 us (23%)
  waiting for transfers between devices  44 us (16%)
  local copies, waits for them, and re-layouts  7.85 us (3%)
    pallas_call x2, Pallas kernels, place(): pl.pallas_call(functools.partial(place_kernel, chunk, width), grid_spec=p...  67.1 us
    ppermute x8, starting transfers between devices, turn(): return [lax.ppermute(blocks[s], ('y', 'x'), pairs(s)) for s in DIGITS]  39.9 us
    all_to_all x1, blocking collectives, gather_weights(): got = lax.all_to_all(spread, 'zh', 0, 0, tiled=True)  36.1 us
    all_to_all x1, blocking collectives, gather_weights(): lax.all_to_all(spread.reshape((16,) + shard.shape[1:]), (axis, 'zh'), 0,...  34.2 us
    all_to_all x1, waiting for transfers between devices, gather_weights(): lax.all_to_all(spread.reshape((16,) + shard.shape[1:]), (axis, 'zh'), 0,...  22.2 us
    ppermute x15, waiting for transfers between devices, shift(): lax.ppermute(array, axis, [(i, (i + by) % size) for i in range(size)])  21.7 us
    pallas_call x6, Pallas kernels, level(): pl.pallas_call(functools.partial(level_kernel, parent_first), grid_spec=p...  21.5 us
    ppermute x15, starting transfers between devices, shift(): lax.ppermute(array, axis, [(i, (i + by) % size) for i in range(size)])  17.2 us
  transfers between devices with their start and end apart: 24, of which 5 were waited for; matrix products, arithmetic and copies ran while one was open for 0% of the time, Pallas kernels for 20%

profile of v1, /device:TPU:24, one launch (start us, length us, event | category | flops | bytes accessed | tf_op | source)
XLA Modules:
  0.0 274.7 jit_solution(17871115399061456694)
XLA Ops:
  1.3 36.1 %all_to_all.15.own_ref = bf16[4,4,4,32,256]{4,3,2,1,0:T(8,128)(2,1)S(1)} all-to-all(bf16[4,4,4,32,256]{4,3,2,1,0:T(8,128)(2,1)S(1)} %broadcast_in_dim.32), channel_id=1, replica_groups=mesh['zl'=2,'y'=4,'x'=4,'zh'=4,'core'=2] {'zh'}, dimensions={0} | all-to-all | bytes 2097152 | tf_op jit(solution)/shard_map/all_to_all | solution.py:106
  37.6 34.2 %all_to_all.16 = bf16[16,4,32,256]{3,2,1,0:T(8,128)(2,1)} all-to-all(bf16[16,4,32,256]{3,2,1,0:T(8,128)(2,1)S(1)} %bitcast.15), channel_id=1, replica_groups=mesh['zl'=2,'y'=4,'x'=4,'zh'=4,'core'=2] {'x','zh'}, dimensions={0} | all-to-all | bytes 2097152 | tf_op jit(solution)/shard_map/all_to_all | solution.py:109
  72.9 5.5 %all-to-all-start = ((bf16[16,4,32,256]{3,2,1,0:T(8,128)(2,1)}), bf16[16,4,32,256]{3,2,1,0:T(8,128)(2,1)}, u32[]{:S(2)}, u32[]{:S(2)}) async-start(bf16[16,4,32,256]{3,2,1,0:T(8,128)(2,1)} %bitcast.14), calls=%async_computation | async-start | bytes 2097152 | tf_op jit(solution)/shard_map/all_to_all | solution.py:109
  78.9 22.2 %all-to-all-done = bf16[16,4,32,256]{3,2,1,0:T(8,128)(2,1)} async-done(((bf16[16,4,32,256]{3,2,1,0:T(8,128)(2,1)}), bf16[16,4,32,256]{3,2,1,0:T(8,128)(2,1)}, u32[]{:S(2)}, u32[]{:S(2)}) %all-to-all-start) | async-done | bytes 1048608 | tf_op jit(solution)/shard_map/all_to_all | solution.py:109
  101.2 3.8 %shard_map.31 = (bf16[256,512]{1,0:T(8,128)(2,1)S(1)}, bf16[256,512]{1,0:T(8,128)(2,1)}, bf16[256,512]{1,0:T(8,128)(2,1)}, bf16[256,512]{1,0:T(8,128)(2,1)}) custom-call(s32[9]{0:T(128)S(1)} %pad_add_fusion.2.order, bf16[4,4,4,32,256]{4,3,2,1,0:T(8,128)(2,1)S(1)} %all_to_all.15.own_ref, bf16[4,4,4,32,256]{4,3,2,1,0:T(8,128)(2,1)} %collective-permute-done.2.other_ref, ...), custom_call_target="tpu_custom_call" | custom-call | flops 1073741824 | bytes 4194304 | tf_op jit(solution)/shard_map/pallas_call | solution.py:43
  108.0 2.6 collective-permute-start.15
  110.7 3.8 %shard_map.28 = (bf16[256,512]{1,0:T(8,128)(2,1)S(1)}, bf16[256,512]{1,0:T(8,128)(2,1)S(1)}, bf16[256,512]{1,0:T(8,128)(2,1)S(1)}, bf16[256,512]{1,0:T(8,128)(2,1)}) custom-call(s32[9]{0:T(128)S(1)} %pad_add_fusion.2.order, bf16[4,4,4,32,256]{4,3,2,1,0:T(8,128)(2,1)S(1)} %all_to_all.15.own_ref, bf16[4,4,4,32,256]{4,3,2,1,0:T(8,128)(2,1)} %collective-permute-done.2.other_ref, ...), custom_call_target="tpu_custom_call" | custom-call | flops 1073741824 | bytes 4194304 | tf_op jit(solution)/shard_map/pallas_call | solution.py:43
  114.5 7.1 %collective-permute-done.13.refs_1_ = bf16[256,512]{1,0:T(8,128)(2,1)} collective-permute-done((bf16[256,512]{1,0:T(8,128)(2,1)}, bf16[256,512]{1,0:T(8,128)(2,1)}, u32[]{:S(2)}, u32[]{:S(2)}) %collective-permute-start.13) | collective-permute-done | bytes 262176 | tf_op jit(solution)/shard_map/ppermute | solution.py:96
  121.6 2.3 collective-permute-start.4
  125.0 3.8 %shard_map.32 = (bf16[256,512]{1,0:T(8,128)(2,1)}, bf16[256,512]{1,0:T(8,128)(2,1)}, bf16[256,512]{1,0:T(8,128)(2,1)S(1)}, bf16[256,512]{1,0:T(8,128)(2,1)S(1)}) custom-call(s32[9]{0:T(128)S(1)} %pad_add_fusion.1.order, bf16[4,4,4,32,256]{4,3,2,1,0:T(8,128)(2,1)S(1)} %bitcast.12, bf16[4,4,4,32,256]{4,3,2,1,0:T(8,128)(2,1)} %collective-permute-done.1.other_ref, ...), custom_call_target="tpu_custom_call" | custom-call | flops 1073741824 | bytes 4194304 | tf_op jit(solution)/shard_map/pallas_call | solution.py:43
  128.8 4.5 %collective-permute-start.16 = (bf16[256,512]{1,0:T(8,128)(2,1)}, bf16[256,512]{1,0:T(8,128)(2,1)S(1)}, u32[]{:S(2)}, u32[]{:S(2)}) collective-permute-start(bf16[256,512]{1,0:T(8,128)(2,1)} %get-tuple-element.45), channel_id=1, source_target_pairs={{0,0},{8,40},{16,80},{24,120},{32,8},{40,48},{48,88},{56,96},{64,1... | collective-permute-start | bytes 786440 | tf_op jit(solution)/shard_map/ppermute | solution.py:121
  133.3 3.1 %collective-permute-done.3.refs_1_ = bf16[256,512]{1,0:T(8,128)(2,1)S(1)} collective-permute-done((bf16[256,512]{1,0:T(8,128)(2,1)S(1)}, bf16[256,512]{1,0:T(8,128)(2,1)S(1)}, u32[]{:S(2)}, u32[]{:S(2)}) %collective-permute-start.3) | collective-permute-done | bytes 262176 | tf_op jit(solution)/shard_map/ppermute | solution.py:96
  136.4 4.3 %collective-permute-start.17 = (bf16[256,512]{1,0:T(8,128)(2,1)}, bf16[256,512]{1,0:T(8,128)(2,1)S(1)}, u32[]{:S(2)}, u32[]{:S(2)}) collective-permute-start(bf16[256,512]{1,0:T(8,128)(2,1)} %get-tuple-element.46), channel_id=1, source_target_pairs={{0,8},{8,48},{16,88},{24,96},{32,16},{40,56},{48,64},{56,104},{64,... | collective-permute-start | bytes 786440 | tf_op jit(solution)/shard_map/ppermute | solution.py:121
  143.3 10.8 %collective-permute-start.19 = (bf16[256,512]{1,0:T(8,128)(2,1)S(1)}, bf16[256,512]{1,0:T(8,128)(2,1)S(1)}, u32[]{:S(2)}, u32[]{:S(2)}) collective-permute-start(bf16[256,512]{1,0:T(8,128)(2,1)S(1)} %get-tuple-element.48), channel_id=1, source_target_pairs={{0,24},{8,32},{16,72},{24,112},{32,0},{40,40},{48,80},{56,120},{64... | collective-permute-start | bytes 786440 | tf_op jit(solution)/shard_map/ppermute | solution.py:121
  155.1 3.1 %shard_map.29 = (bf16[256,512]{1,0:T(8,128)(2,1)S(1)}, bf16[256,512]{1,0:T(8,128)(2,1)S(1)}, bf16[256,512]{1,0:T(8,128)(2,1)S(1)}, bf16[256,512]{1,0:T(8,128)(2,1)S(1)}) custom-call(s32[9]{0:T(128)S(1)} %pad_add_fusion.1.order, bf16[4,4,4,32,256]{4,3,2,1,0:T(8,128)(2,1)S(1)} %bitcast.13, bf16[4,4,4,32,256]{4,3,2,1,0:T(8,128)(2,1)} %collective-permute-done.1.other_ref, ...), custom_call_target="tpu_custom_call" | custom-call | flops 1073741824 | bytes 4194304 | tf_op jit(solution)/shard_map/pallas_call | solution.py:43
  164.0 12.7 %collective-permute-start.9 = (bf16[256,512]{1,0:T(8,128)(2,1)S(1)}, bf16[256,512]{1,0:T(8,128)(2,1)S(1)}, u32[]{:S(2)}, u32[]{:S(2)}) collective-permute-start(bf16[256,512]{1,0:T(8,128)(2,1)S(1)} %get-tuple-element.36), channel_id=1, source_target_pairs={{0,24},{8,32},{16,72},{24,112},{32,0},{40,40},{48,80},{56,120},{64... | collective-permute-start | bytes 786440 | tf_op jit(solution)/shard_map/ppermute | solution.py:121
  176.8 3.4 %shard_map.33 = (bf16[256,512]{1,0:T(8,128)(2,1)S(1)}, bf16[256,512]{1,0:T(8,128)(2,1)S(1)}, bf16[256,512]{1,0:T(8,128)(2,1)S(1)}, bf16[256,512]{1,0:T(8,128)(2,1)S(1)}) custom-call(s32[9]{0:T(128)S(1)} %pad_add_fusion.order, bf16[4,4,4,32,256]{4,3,2,1,0:T(8,128)(2,1)} %bitcast.3.own_ref, bf16[4,4,4,32,256]{4,3,2,1,0:T(8,128)(2,1)} %collective-permute-done.other_ref, ...), custom_call_target="tpu_custom_call" | custom-call | flops 1073741824 | bytes 4194304 | tf_op jit(solution)/shard_map/pallas_call | solution.py:43
  181.0 3.5 %shard_map.30 = (bf16[256,512]{1,0:T(8,128)(2,1)S(1)}, bf16[256,512]{1,0:T(8,128)(2,1)S(1)}, bf16[256,512]{1,0:T(8,128)(2,1)S(1)}, bf16[256,512]{1,0:T(8,128)(2,1)S(1)}) custom-call(s32[9]{0:T(128)S(1)} %pad_add_fusion.order, bf16[4,4,4,32,256]{4,3,2,1,0:T(8,128)(2,1)} %bitcast.3.own_ref, bf16[4,4,4,32,256]{4,3,2,1,0:T(8,128)(2,1)} %collective-permute-done.other_ref, ...), custom_call_target="tpu_custom_call" | custom-call | flops 1073741824 | bytes 4194304 | tf_op jit(solution)/shard_map/pallas_call | solution.py:43
  186.2 3.4 %collective-permute-start.21 = (bf16[256,512]{1,0:T(8,128)(2,1)S(1)}, bf16[256,512]{1,0:T(8,128)(2,1)S(1)}, u32[]{:S(2)}, u32[]{:S(2)}) collective-permute-start(bf16[256,512]{1,0:T(8,128)(2,1)S(1)} %get-tuple-element.51), channel_id=1, source_target_pairs={{0,64},{32,96},{64,0},{96,32},{1,65},{33,97},{65,1},{97,33},{2,66}... | collective-permute-start | bytes 786440 | tf_op jit(solution)/shard_map/ppermute | solution.py:96
  191.6 2.1 collective-permute-start.12
  194.2 2.6 collective-permute-done.21.refs_2_
  196.9 8.9 %collective-permute-done.22.refs_3_ = bf16[256,512]{1,0:T(8,128)(2,1)S(1)} collective-permute-done((bf16[256,512]{1,0:T(8,128)(2,1)S(1)}, bf16[256,512]{1,0:T(8,128)(2,1)S(1)}, u32[]{:S(2)}, u32[]{:S(2)}) %collective-permute-start.22) | collective-permute-done | bytes 262176 | tf_op jit(solution)/shard_map/ppermute | solution.py:96
  206.5 33.6 %shard_map.34.refs_4_ = bf16[4,256,1024]{2,1,0:T(8,128)(2,1)} custom-call(s32[4]{0:T(128)} %and_select_fusion.6.order, bf16[256,512]{1,0:T(8,128)(2,1)} %copy-done.3, bf16[256,512]{1,0:T(8,128)(2,1)} %copy-done.9, bf16[256,512]{1,0:T(8,128)(2,1)} %copy-done.10, bf16[256,512]{1,0:T(8,128)(2,1)} %copy-done.11), custom_call_target="tpu_custom_call" | custom-call | tf_op jit(solution)/shard_map/pallas_call | solution.py:80
  241.0 33.6 %shard_map.35 = bf16[4,256,1024]{2,1,0:T(8,128)(2,1)} custom-call(s32[4]{0:T(128)} %and_select_fusion.6.order, bf16[256,512]{1,0:T(8,128)(2,1)} %copy-done.4, bf16[256,512]{1,0:T(8,128)(2,1)} %copy-done.12, bf16[256,512]{1,0:T(8,128)(2,1)} %copy-done.13, bf16[256,512]{1,0:T(8,128)(2,1)} %copy-done.14, ...), custom_call_target="tpu_custom_call", output_to_operand_aliasing={{}: (5, {})} | custom-call | tf_op jit(solution)/shard_map/pallas_call | solution.py:80
  (75 shorter events, 23.3 us)
Async XLA Ops:
  72.9 28.2 %all-to-all-start = ((bf16[16,4,32,256]{3,2,1,0:T(8,128)(2,1)}), bf16[16,4,32,256]{3,2,1,0:T(8,128)(2,1)}, u32[]{:S(2)}, u32[]{:S(2)}) async-start(bf16[16,4,32,256]{3,2,1,0:T(8,128)(2,1)} %bitcast.14), calls=%async_computation | async-start | bytes 2097152 | tf_op jit(solution)/shard_map/all_to_all | solution.py:109
  78.4 22.8 %collective-permute-start.2 = (bf16[4,4,4,32,256]{4,3,2,1,0:T(8,128)(2,1)S(1)}, bf16[4,4,4,32,256]{4,3,2,1,0:T(8,128)(2,1)}, u32[]{:S(2)}, u32[]{:S(2)}) collective-permute-start(bf16[4,4,4,32,256]{4,3,2,1,0:T(8,128)(2,1)S(1)} %all_to_all.15.own_ref), channel_id=1, source_target_pairs={{0,1},{1,0},{2,3},{3,2},{4,5},{5,4},{6,7},{7,6},{8,9},{9,8},{10,11... | collective-permute-start | bytes 3145736 | tf_op jit(solution)/shard_map/ppermute | solution.py:96
  78.4 46.6 %collective-permute-start.1 = (bf16[4,4,4,32,256]{4,3,2,1,0:T(8,128)(2,1)}, bf16[4,4,4,32,256]{4,3,2,1,0:T(8,128)(2,1)}, u32[]{:S(2)}, u32[]{:S(2)}) collective-permute-start(bf16[4,4,4,32,256]{4,3,2,1,0:T(8,128)(2,1)} %bitcast.11), channel_id=1, source_target_pairs={{0,1},{1,0},{2,3},{3,2},{4,5},{5,4},{6,7},{7,6},{8,9},{9,8},{10,11... | collective-permute-start | bytes 3145736 | tf_op jit(solution)/shard_map/ppermute | solution.py:96
  101.1 57.1 %collective-permute-start = (bf16[4,4,4,32,256]{4,3,2,1,0:T(8,128)(2,1)}, bf16[4,4,4,32,256]{4,3,2,1,0:T(8,128)(2,1)}, u32[]{:S(2)}, u32[]{:S(2)}) collective-permute-start(bf16[4,4,4,32,256]{4,3,2,1,0:T(8,128)(2,1)} %bitcast.3.own_ref), channel_id=1, source_target_pairs={{0,1},{1,0},{2,3},{3,2},{4,5},{5,4},{6,7},{7,6},{8,9},{9,8},{10,11... | collective-permute-start | bytes 3145736 | tf_op jit(solution)/shard_map/ppermute | solution.py:96
  105.7 15.9 %collective-permute-start.13 = (bf16[256,512]{1,0:T(8,128)(2,1)}, bf16[256,512]{1,0:T(8,128)(2,1)}, u32[]{:S(2)}, u32[]{:S(2)}) collective-permute-start(bf16[256,512]{1,0:T(8,128)(2,1)} %get-tuple-element.42), channel_id=1, source_target_pairs={{0,8},{8,16},{16,24},{24,0},{1,9},{9,17},{17,25},{25,1},{2,10},{10... | collective-permute-start | bytes 786440 | tf_op jit(solution)/shard_map/ppermute | solution.py:96
  107.7 13.9 %collective-permute-start.14 = (bf16[256,512]{1,0:T(8,128)(2,1)}, bf16[256,512]{1,0:T(8,128)(2,1)}, u32[]{:S(2)}, u32[]{:S(2)}) collective-permute-start(bf16[256,512]{1,0:T(8,128)(2,1)} %get-tuple-element.43), channel_id=1, source_target_pairs={{0,16},{8,24},{16,0},{24,8},{1,17},{9,25},{17,1},{25,9},{2,18},{10... | collective-permute-start | bytes 786440 | tf_op jit(solution)/shard_map/ppermute | solution.py:96
  108.0 15.9 %collective-permute-start.15 = (bf16[256,512]{1,0:T(8,128)(2,1)}, bf16[256,512]{1,0:T(8,128)(2,1)}, u32[]{:S(2)}, u32[]{:S(2)}) collective-permute-start(bf16[256,512]{1,0:T(8,128)(2,1)} %get-tuple-element.44), channel_id=1, source_target_pairs={{0,24},{8,0},{16,8},{24,16},{1,25},{9,1},{17,9},{25,17},{2,26},{10... | collective-permute-start | bytes 786440 | tf_op jit(solution)/shard_map/ppermute | solution.py:96
  121.6 14.8 %collective-permute-start.3 = (bf16[256,512]{1,0:T(8,128)(2,1)S(1)}, bf16[256,512]{1,0:T(8,128)(2,1)S(1)}, u32[]{:S(2)}, u32[]{:S(2)}) collective-permute-start(bf16[256,512]{1,0:T(8,128)(2,1)S(1)} %get-tuple-element.30), channel_id=1, source_target_pairs={{0,8},{8,16},{16,24},{24,0},{1,9},{9,17},{17,25},{25,1},{2,10},{10... | collective-permute-start | bytes 786440 | tf_op jit(solution)/shard_map/ppermute | solution.py:96
  121.6 19.0 %collective-permute-start.4 = (bf16[256,512]{1,0:T(8,128)(2,1)S(1)}, bf16[256,512]{1,0:T(8,128)(2,1)S(1)}, u32[]{:S(2)}, u32[]{:S(2)}) collective-permute-start(bf16[256,512]{1,0:T(8,128)(2,1)S(1)} %get-tuple-element.31), channel_id=1, source_target_pairs={{0,16},{8,24},{16,0},{24,8},{1,17},{9,25},{17,1},{25,9},{2,18},{10... | collective-permute-start | bytes 786440 | tf_op jit(solution)/shard_map/ppermute | solution.py:96
  123.9 18.6 %collective-permute-start.5 = (bf16[256,512]{1,0:T(8,128)(2,1)}, bf16[256,512]{1,0:T(8,128)(2,1)S(1)}, u32[]{:S(2)}, u32[]{:S(2)}) collective-permute-start(bf16[256,512]{1,0:T(8,128)(2,1)} %get-tuple-element.32), channel_id=1, source_target_pairs={{0,24},{8,0},{16,8},{24,16},{1,25},{9,1},{17,9},{25,17},{2,26},{10... | collective-permute-start | bytes 786440 | tf_op jit(solution)/shard_map/ppermute | solution.py:96
  128.8 31.3 %collective-permute-start.16 = (bf16[256,512]{1,0:T(8,128)(2,1)}, bf16[256,512]{1,0:T(8,128)(2,1)S(1)}, u32[]{:S(2)}, u32[]{:S(2)}) collective-permute-start(bf16[256,512]{1,0:T(8,128)(2,1)} %get-tuple-element.45), channel_id=1, source_target_pairs={{0,0},{8,40},{16,80},{24,120},{32,8},{40,48},{48,88},{56,96},{64,1... | collective-permute-start | bytes 786440 | tf_op jit(solution)/shard_map/ppermute | solution.py:121
  136.4 25.7 %collective-permute-start.17 = (bf16[256,512]{1,0:T(8,128)(2,1)}, bf16[256,512]{1,0:T(8,128)(2,1)S(1)}, u32[]{:S(2)}, u32[]{:S(2)}) collective-permute-start(bf16[256,512]{1,0:T(8,128)(2,1)} %get-tuple-element.46), channel_id=1, source_target_pairs={{0,8},{8,48},{16,88},{24,96},{32,16},{40,56},{48,64},{56,104},{64,... | collective-permute-start | bytes 786440 | tf_op jit(solution)/shard_map/ppermute | solution.py:121
  140.6 23.4 %collective-permute-start.18 = (bf16[256,512]{1,0:T(8,128)(2,1)S(1)}, bf16[256,512]{1,0:T(8,128)(2,1)S(1)}, u32[]{:S(2)}, u32[]{:S(2)}) collective-permute-start(bf16[256,512]{1,0:T(8,128)(2,1)S(1)} %get-tuple-element.47), channel_id=1, source_target_pairs={{0,16},{8,56},{16,64},{24,104},{32,24},{40,32},{48,72},{56,112},{6... | collective-permute-start | bytes 786440 | tf_op jit(solution)/shard_map/ppermute | solution.py:121
  143.3 33.5 %collective-permute-start.19 = (bf16[256,512]{1,0:T(8,128)(2,1)S(1)}, bf16[256,512]{1,0:T(8,128)(2,1)S(1)}, u32[]{:S(2)}, u32[]{:S(2)}) collective-permute-start(bf16[256,512]{1,0:T(8,128)(2,1)S(1)} %get-tuple-element.48), channel_id=1, source_target_pairs={{0,24},{8,32},{16,72},{24,112},{32,0},{40,40},{48,80},{56,120},{64... | collective-permute-start | bytes 786440 | tf_op jit(solution)/shard_map/ppermute | solution.py:121
  158.2 22.8 %collective-permute-start.6 = (bf16[256,512]{1,0:T(8,128)(2,1)S(1)}, bf16[256,512]{1,0:T(8,128)(2,1)S(1)}, u32[]{:S(2)}, u32[]{:S(2)}) collective-permute-start(bf16[256,512]{1,0:T(8,128)(2,1)S(1)} %get-tuple-element.33), channel_id=1, source_target_pairs={{0,0},{8,40},{16,80},{24,120},{32,8},{40,48},{48,88},{56,96},{64,1... | collective-permute-start | bytes 786440 | tf_op jit(solution)/shard_map/ppermute | solution.py:121
  160.2 20.8 %collective-permute-start.7 = (bf16[256,512]{1,0:T(8,128)(2,1)S(1)}, bf16[256,512]{1,0:T(8,128)(2,1)S(1)}, u32[]{:S(2)}, u32[]{:S(2)}) collective-permute-start(bf16[256,512]{1,0:T(8,128)(2,1)S(1)} %get-tuple-element.34), channel_id=1, source_target_pairs={{0,8},{8,48},{16,88},{24,96},{32,16},{40,56},{48,64},{56,104},{64,... | collective-permute-start | bytes 786440 | tf_op jit(solution)/shard_map/ppermute | solution.py:121
  162.1 18.9 %collective-permute-start.8 = (bf16[256,512]{1,0:T(8,128)(2,1)S(1)}, bf16[256,512]{1,0:T(8,128)(2,1)S(1)}, u32[]{:S(2)}, u32[]{:S(2)}) collective-permute-start(bf16[256,512]{1,0:T(8,128)(2,1)S(1)} %get-tuple-element.35), channel_id=1, source_target_pairs={{0,16},{8,56},{16,64},{24,104},{32,24},{40,32},{48,72},{56,112},{6... | collective-permute-start | bytes 786440 | tf_op jit(solution)/shard_map/ppermute | solution.py:121
  164.0 17.0 %collective-permute-start.9 = (bf16[256,512]{1,0:T(8,128)(2,1)S(1)}, bf16[256,512]{1,0:T(8,128)(2,1)S(1)}, u32[]{:S(2)}, u32[]{:S(2)}) collective-permute-start(bf16[256,512]{1,0:T(8,128)(2,1)S(1)} %get-tuple-element.36), channel_id=1, source_target_pairs={{0,24},{8,32},{16,72},{24,112},{32,0},{40,40},{48,80},{56,120},{64... | collective-permute-start | bytes 786440 | tf_op jit(solution)/shard_map/ppermute | solution.py:121
  181.0 10.6 %collective-permute-start.20 = (bf16[256,512]{1,0:T(8,128)(2,1)S(1)}, bf16[256,512]{1,0:T(8,128)(2,1)S(1)}, u32[]{:S(2)}, u32[]{:S(2)}) collective-permute-start(bf16[256,512]{1,0:T(8,128)(2,1)S(1)} %get-tuple-element.50), channel_id=1, source_target_pairs={{0,32},{32,64},{64,96},{96,0},{1,33},{33,65},{65,97},{97,1},{2,34}... | collective-permute-start | bytes 786440 | tf_op jit(solution)/shard_map/ppermute | solution.py:96
  185.2 54.9 %collective-permute-start.10 = (bf16[256,512]{1,0:T(8,128)(2,1)S(1)}, bf16[256,512]{1,0:T(8,128)(2,1)S(1)}, u32[]{:S(2)}, u32[]{:S(2)}) collective-permute-start(bf16[256,512]{1,0:T(8,128)(2,1)S(1)} %get-tuple-element.38), channel_id=1, source_target_pairs={{0,32},{32,64},{64,96},{96,0},{1,33},{33,65},{65,97},{97,1},{2,34}... | collective-permute-start | bytes 786440 | tf_op jit(solution)/shard_map/ppermute | solution.py:96
  186.2 10.7 %collective-permute-start.21 = (bf16[256,512]{1,0:T(8,128)(2,1)S(1)}, bf16[256,512]{1,0:T(8,128)(2,1)S(1)}, u32[]{:S(2)}, u32[]{:S(2)}) collective-permute-start(bf16[256,512]{1,0:T(8,128)(2,1)S(1)} %get-tuple-element.51), channel_id=1, source_target_pairs={{0,64},{32,96},{64,0},{96,32},{1,65},{33,97},{65,1},{97,33},{2,66}... | collective-permute-start | bytes 786440 | tf_op jit(solution)/shard_map/ppermute | solution.py:96
  189.5 16.3 %collective-permute-start.22 = (bf16[256,512]{1,0:T(8,128)(2,1)S(1)}, bf16[256,512]{1,0:T(8,128)(2,1)S(1)}, u32[]{:S(2)}, u32[]{:S(2)}) collective-permute-start(bf16[256,512]{1,0:T(8,128)(2,1)S(1)} %get-tuple-element.52), channel_id=1, source_target_pairs={{0,96},{32,0},{64,32},{96,64},{1,97},{33,1},{65,33},{97,65},{2,98}... | collective-permute-start | bytes 786440 | tf_op jit(solution)/shard_map/ppermute | solution.py:96
  191.0 49.1 %collective-permute-start.11 = (bf16[256,512]{1,0:T(8,128)(2,1)S(1)}, bf16[256,512]{1,0:T(8,128)(2,1)S(1)}, u32[]{:S(2)}, u32[]{:S(2)}) collective-permute-start(bf16[256,512]{1,0:T(8,128)(2,1)S(1)} %get-tuple-element.39), channel_id=1, source_target_pairs={{0,64},{32,96},{64,0},{96,32},{1,65},{33,97},{65,1},{97,33},{2,66}... | collective-permute-start | bytes 786440 | tf_op jit(solution)/shard_map/ppermute | solution.py:96
  191.6 48.5 %collective-permute-start.12 = (bf16[256,512]{1,0:T(8,128)(2,1)S(1)}, bf16[256,512]{1,0:T(8,128)(2,1)S(1)}, u32[]{:S(2)}, u32[]{:S(2)}) collective-permute-start(bf16[256,512]{1,0:T(8,128)(2,1)S(1)} %get-tuple-element.40), channel_id=1, source_target_pairs={{0,96},{32,0},{64,32},{96,64},{1,97},{33,1},{65,33},{97,65},{2,98}... | collective-permute-start | bytes 786440 | tf_op jit(solution)/shard_map/ppermute | solution.py:96
  (15 other events, 127.8 us)

commit v2 on v1

v2 whole, which is shorter than its diff:
```python
import functools

import jax
import jax.numpy as jnp
from jax import lax
from jax.experimental import pallas as pl
from jax.experimental.pallas import tpu as pltpu
from jax.sharding import Mesh, PartitionSpec as P

DIGITS = range(4)
CHUNKS = 2
VMEM, ALL_VMEM = 20 * 2**20, 60 * 2**20


def assemble(pieces, order, held, weights):
    core, own_zh = order[0], order[1]
    for (behind, other), ref in zip(pieces, held):
        half = 1 - core if other else core
        at = lax.rem(own_zh - behind + 4, 4)
        rows = pl.ds(pl.multiple_of(64 * at + 32 * half, 32), 32)
        weights[:, :, rows, :] = ref[...]


def level_kernel(pieces, order, *refs):
    if pieces:
        held, refs, weights = refs[: len(pieces)], refs[len(pieces) : -1], refs[-1]
        assemble(pieces, order, held, weights)
    else:
        weights, refs = refs[0], refs[1:]
    children, outs = refs[:-4], refs[-4:]
    blocks = [children[0].at[order[6 + p]] for p in DIGITS] if len(children) == 1 else children
    for s in DIGITS:
        total = sum(
            jnp.dot(
                weights[order[2 + s], order[6 + p]],
                blocks[p][...],
                preferred_element_type=jnp.float32,
            )
            for p in DIGITS
        )
        outs[s][...] = total.astype(outs[s].dtype)


def level(order, held, children, pieces=(), chunk=None, vmem=VMEM):
    whole = lambda a: pl.BlockSpec(a.shape, lambda i, o: (0,) * a.ndim)
    operands = list(held) + list(children)
    width = children[0].shape[-1]
    specs = [whole(a) for a in operands]
    if chunk is not None:
        width //= CHUNKS
        specs[-1] = pl.BlockSpec((4, 256, width), lambda i, o: (0, 0, chunk))
    return pl.pallas_call(
        functools.partial(level_kernel, pieces),
        grid_spec=pltpu.PrefetchScalarGridSpec(
            num_scalar_prefetch=1,
            grid=(1,),
            in_specs=specs,
            out_specs=[pl.BlockSpec((256, width), lambda i, o: (0, 0))] * 4,
            scratch_shapes=[pltpu.VMEM((4, 4, 256, 256), jnp.bfloat16)] if pieces else [],
        ),
        out_shape=[jax.ShapeDtypeStruct((256, width), jnp.bfloat16)] * 4,
        cost_estimate=pl.CostEstimate(
            flops=2 * 16 * 256 * 256 * width,
            bytes_accessed=2 * (16 * 256 * 256 + 8 * 256 * width),
            transcendentals=0,
        ),
        compiler_params=pltpu.CompilerParams(vmem_limit_bytes=vmem),
    )(order, *operands)


def place_kernel(order, *refs):
    blocks, out = refs[:4], refs[-1]
    for s in DIGITS:
        @pl.when(pl.program_id(0) == s)
        def _():
            out[0] = blocks[s][...]


def place(order, blocks, chunk, into):
    rows, width = blocks[0].shape
    extra = [] if into is None else [into]
    return pl.pallas_call(
        place_kernel,
        grid_spec=pltpu.PrefetchScalarGridSpec(
            num_scalar_prefetch=1,
            grid=(4,),
            in_specs=[pl.BlockSpec((rows, width), lambda i, o: (0, 0))] * 4
            + [pl.BlockSpec(memory_space=pl.ANY)] * len(extra),
            out_specs=pl.BlockSpec((1, rows, width), lambda i, o: (o[i], 0, chunk)),
        ),
        out_shape=jax.ShapeDtypeStruct((4, rows, CHUNKS * width), jnp.bfloat16),
        input_output_aliases={5: 0} if extra else {},
        compiler_params=pltpu.CompilerParams(vmem_limit_bytes=VMEM),
    )(order, *blocks, *extra)


def select_kernel(order, *refs):
    blocks, outs = refs[:4], refs[4:]
    for t in DIGITS:
        for s in DIGITS:
            @pl.when(order[t] == s)
            def _():
                outs[t][...] = blocks[s][...]


def select(order, blocks):
    whole = pl.BlockSpec(blocks[0].shape, lambda i, o: (0, 0))
    return pl.pallas_call(
        select_kernel,
        grid_spec=pltpu.PrefetchScalarGridSpec(
            num_scalar_prefetch=1, grid=(1,), in_specs=[whole] * 4, out_specs=[whole] * 4
        ),
        out_shape=[jax.ShapeDtypeStruct(a.shape, a.dtype) for a in blocks],
        compiler_params=pltpu.CompilerParams(vmem_limit_bytes=VMEM),
    )(order, *blocks)


def shift(array, axis, by):
    size = lax.axis_size(axis)
    return lax.ppermute(array, axis, [(i, (i + by) % size) for i in range(size)])


def swap(array):
    return shift(array, "core", 1)


def after(value, *others):
    return lax.optimization_barrier((value,) + others)[0]


BEHIND = (0, 1, 3, 2)
PIECES = tuple((behind, other) for behind in BEHIND for other in (0, 1))


def z_pieces(shard):
    return [shard] + [shift(shard, "zh", behind) for behind in BEHIND[1:]]


def both_cores(pieces):
    return [array for own in pieces for array in (own, swap(own))]


def exchange(blocks, axis):
    return [blocks[0]] + [shift(blocks[s], axis, s) for s in (1, 2, 3)]


def hand_over(shard, axis):
    return lax.all_to_all(shard, axis, 0, 0, tiled=True)


def all_rows(mine):
    return lax.all_gather(mine, ("zh", "core"), axis=2, tiled=True)


def local(coefficients, transfer):
    a, b = lax.axis_index("x"), lax.axis_index("y")
    zh, core = lax.axis_index("zh"), lax.axis_index("core")
    steps = jnp.arange(4, dtype=jnp.int32)

    def order(slots, children):
        head = jnp.stack([core, zh])
        return jnp.concatenate([head, slots % 4, children % 4]).astype(jnp.int32)

    order0 = order(a + steps, steps)
    order1 = order(a + steps, a - steps + 4)
    order2 = order(b + steps, b - steps + 4)
    orders = ((a - b - steps + 8) % 4).astype(jnp.int32)
    orderp = ((b - steps + 4) % 4).astype(jnp.int32)

    pieces = z_pieces(transfer[0])
    first = swap(pieces[0])
    mine1 = hand_over(after(transfer[1], first), "x")
    mine2 = hand_over(after(transfer[2], mine1), "y")
    *near, mine1, mine2 = lax.optimization_barrier((*pieces[1:3], mine1, mine2))
    w0 = [pieces[0], first] + both_cores(near + pieces[3:])
    w1 = all_rows(after(mine1, *near))
    w2 = all_rows(after(mine2, *w0))
    states = [
        exchange(level(order0, w0, [coefficients], PIECES, c, ALL_VMEM), "x") for c in range(CHUNKS)
    ]
    for c in range(CHUNKS):
        memory = VMEM if c else ALL_VMEM
        states[c] = exchange(level(order1, [w1], states[c], vmem=memory), "x")
        states[c] = exchange(select(orders, states[c]), "y")
    for c in range(CHUNKS):
        states[c] = exchange(level(order2, [w2], states[c]), "y")
    result = None
    for c in range(CHUNKS):
        result = place(orderp, states[c], c, result)
    return result


def solution(mesh):
    fine = Mesh(mesh.devices.reshape(2, 4, 4, 4, 2), ("zl", "y", "x", "zh", "core"))
    node, col = ("zl", "y", "x"), ("zh", "core")
    return jax.shard_map(
        local,
        mesh=fine,
        in_specs=(P(node, None, col), P(None, node, None, col, None)),
        out_specs=P(node, None, col),
        check_vma=False,
    )
```

time: 275 us -> 166 us (0.60)
  the two profiles are of different devices: /device:TPU:24 before, /device:TPU:62 now
where the time goes in v2:
time: 166 us; the launch traced here: 164 us
  waiting for transfers between devices  66.7 us (40%)
  starting transfers between devices  50.2 us (30%)
  Pallas kernels  26.3 us (16%)
  between operations  13.6 us (8%)
  local copies, waits for them, and re-layouts  5.95 us (4%)
    ppermute x31, waiting for transfers between devices, shift(): lax.ppermute(array, axis, [(i, (i + by) % size) for i in range(size)])  66.7 us
    ppermute x31, starting transfers between devices, shift(): lax.ppermute(array, axis, [(i, (i + by) % size) for i in range(size)])  40.7 us
    pallas_call x6, Pallas kernels, level(): pl.pallas_call(functools.partial(level_kernel, pieces), grid_spec=pltpu.P...  19.9 us
    all_to_all x2, starting transfers between devices, hand_over(): return lax.all_to_all(shard, axis, 0, 0, tiled=True)  9.45 us
    pallas_call x2, Pallas kernels, place(): pl.pallas_call(place_kernel, grid_spec=pltpu.PrefetchScalarGridSpec(num_s...  4.23 us
    unnamed x38, local copies, waits for them, and re-layouts  3.98 us
  transfers between devices with their start and end apart: 35, of which 16 were waited for; matrix products, arithmetic and copies ran while one was open for 0% of the time, Pallas kernels for 15%

profile of v2, /device:TPU:62, one launch (start us, length us, event | category | flops | bytes accessed | tf_op | source)
XLA Modules:
  0.0 163.5 jit_solution(14140967481880941473)
XLA Ops:
  10.0 4.8 %all-to-all-start = ((bf16[4,4,32,256]{3,2,1,0:T(8,128)(2,1)}), bf16[4,4,32,256]{3,2,1,0:T(8,128)(2,1)S(1)}, u32[]{:S(2)}, u32[]{:S(2)}) async-start(bf16[4,4,32,256]{3,2,1,0:T(8,128)(2,1)} %get-tuple-element.45), calls=%async_computation | async-start | bytes 524288 | tf_op jit(solution)/shard_map/all_to_all | solution.py:148
  14.8 3.3 %collective-permute-start = (bf16[4,4,32,256]{3,2,1,0:T(8,128)(2,1)S(1)}, bf16[4,4,32,256]{3,2,1,0:T(8,128)(2,1)S(1)}, u32[]{:S(2)}, u32[]{:S(2)}) collective-permute-start(bf16[4,4,32,256]{3,2,1,0:T(8,128)(2,1)S(1)} %get-tuple-element.86.refs_0_), channel_id=1, source_target_pairs={{0,2},{2,4},{4,6},{6,0},{1,3},{3,5},{5,7},{7,1},{8,10},{10,12},{12... | collective-permute-start | bytes 786440 | tf_op jit(solution)/shard_map/ppermute | solution.py:120
  18.1 2.1 %collective-permute-start.1 = (bf16[4,4,32,256]{3,2,1,0:T(8,128)(2,1)S(1)}, bf16[4,4,32,256]{3,2,1,0:T(8,128)(2,1)S(1)}, u32[]{:S(2)}, u32[]{:S(2)}) collective-permute-start(bf16[4,4,32,256]{3,2,1,0:T(8,128)(2,1)S(1)} %get-tuple-element.86.refs_0_), channel_id=1, source_target_pairs={{0,6},{2,0},{4,2},{6,4},{1,7},{3,1},{5,3},{7,5},{8,14},{10,8},{12,... | collective-permute-start | bytes 786440 | tf_op jit(solution)/shard_map/ppermute | solution.py:120
  20.2 4.7 %all-to-all-start.1 = ((bf16[4,4,32,256]{3,2,1,0:T(8,128)(2,1)}), bf16[4,4,32,256]{3,2,1,0:T(8,128)(2,1)S(1)}, u32[]{:S(2)}, u32[]{:S(2)}) async-start(bf16[4,4,32,256]{3,2,1,0:T(8,128)(2,1)} %get-tuple-element.46), calls=%async_computation.1 | async-start | bytes 524288 | tf_op jit(solution)/shard_map/all_to_all | solution.py:148
  24.9 7.0 %collective-permute-done.refs_2_ = bf16[4,4,32,256]{3,2,1,0:T(8,128)(2,1)S(1)} collective-permute-done((bf16[4,4,32,256]{3,2,1,0:T(8,128)(2,1)S(1)}, bf16[4,4,32,256]{3,2,1,0:T(8,128)(2,1)S(1)}, u32[]{:S(2)}, u32[]{:S(2)}) %collective-permute-start) | collective-permute-done | bytes 262176 | tf_op jit(solution)/shard_map/ppermute | solution.py:120
  32.0 3.5 %collective-permute-start.5 = (bf16[4,4,32,256]{3,2,1,0:T(8,128)(2,1)S(1)}, bf16[4,4,32,256]{3,2,1,0:T(8,128)(2,1)S(1)}, u32[]{:S(2)}, u32[]{:S(2)}) collective-permute-start(bf16[4,4,32,256]{3,2,1,0:T(8,128)(2,1)S(1)} %get-tuple-element.86.refs_0_), channel_id=1, source_target_pairs={{0,4},{2,6},{4,0},{6,2},{1,5},{3,7},{5,1},{7,3},{8,12},{10,14},{12... | collective-permute-start | bytes 786440 | tf_op jit(solution)/shard_map/ppermute | solution.py:120
  35.5 13.4 %collective-permute-done.5.refs_6_ = bf16[4,4,32,256]{3,2,1,0:T(8,128)(2,1)S(1)} collective-permute-done((bf16[4,4,32,256]{3,2,1,0:T(8,128)(2,1)S(1)}, bf16[4,4,32,256]{3,2,1,0:T(8,128)(2,1)S(1)}, u32[]{:S(2)}, u32[]{:S(2)}) %collective-permute-start.5) | collective-permute-done | bytes 262176 | tf_op jit(solution)/shard_map/ppermute | solution.py:120
  51.9 4.6 %shard_map.32 = (bf16[256,512]{1,0:T(8,128)(2,1)}, bf16[256,512]{1,0:T(8,128)(2,1)}, bf16[256,512]{1,0:T(8,128)(2,1)}, bf16[256,512]{1,0:T(8,128)(2,1)}) custom-call(s32[10]{0:T(128)} %get-tuple-element.88.order, bf16[4,4,32,256]{3,2,1,0:T(8,128)(2,1)} %copy-done.6, bf16[4,4,32,256]{3,2,1,0:T(8,128)(2,1)} %copy-done.7, bf16[4,4,32,256]{3,2,1,0:T(8,128)(2,1)} %copy-done.8, ...), custom_call_target="tpu_custom_call" | custom-call | flops 1073741824 | bytes 4194304 | tf_op jit(solution)/shard_map/pallas_call | solution.py:52
  59.5 4.6 %shard_map.28 = (bf16[256,512]{1,0:T(8,128)(2,1)}, bf16[256,512]{1,0:T(8,128)(2,1)}, bf16[256,512]{1,0:T(8,128)(2,1)}, bf16[256,512]{1,0:T(8,128)(2,1)}) custom-call(s32[10]{0:T(128)} %get-tuple-element.88.order, bf16[4,4,32,256]{3,2,1,0:T(8,128)(2,1)} %copy-done.6, bf16[4,4,32,256]{3,2,1,0:T(8,128)(2,1)} %copy-done.7, bf16[4,4,32,256]{3,2,1,0:T(8,128)(2,1)} %copy-done.8, ...), custom_call_target="tpu_custom_call" | custom-call | flops 1073741824 | bytes 4194304 | tf_op jit(solution)/shard_map/pallas_call | solution.py:52
  64.1 3.4 %collective-permute-start.7 = (bf16[256,512]{1,0:T(8,128)(2,1)}, bf16[256,512]{1,0:T(8,128)(2,1)S(1)}, u32[]{:S(2)}, u32[]{:S(2)}) collective-permute-start(bf16[256,512]{1,0:T(8,128)(2,1)} %get-tuple-element.54), channel_id=1, source_target_pairs={{0,8},{8,16},{16,24},{24,0},{1,9},{9,17},{17,25},{25,1},{2,10},{10... | collective-permute-start | bytes 786440 | tf_op jit(solution)/shard_map/ppermute | solution.py:120
  68.9 5.2 %collective-permute-done.21.refs_4_ = bf16[256,512]{1,0:T(8,128)(2,1)S(1)} collective-permute-done((bf16[256,512]{1,0:T(8,128)(2,1)}, bf16[256,512]{1,0:T(8,128)(2,1)S(1)}, u32[]{:S(2)}, u32[]{:S(2)}) %collective-permute-start.21) | collective-permute-done | bytes 262176 | tf_op jit(solution)/shard_map/ppermute | solution.py:120
  74.9 4.4 %shard_map.33 = (bf16[256,512]{1,0:T(8,128)(2,1)}, bf16[256,512]{1,0:T(8,128)(2,1)}, bf16[256,512]{1,0:T(8,128)(2,1)}, bf16[256,512]{1,0:T(8,128)(2,1)}) custom-call(s32[10]{0:T(128)} %get-tuple-element.89.order, bf16[4,4,256,256]{3,2,1,0:T(8,128)(2,1)} %all-gather.5.cloned.1.call-done.refs_0_, bf16[256,512]{1,0:T(8,128)(2,1)} %get-tuple-element.69.refs_1_, ...), custom_call_target="tpu_custom_call" | custom-call | flops 1073741824 | bytes 4194304 | tf_op jit(solution)/shard_map/pallas_call | solution.py:52
  79.8 5.1 %collective-permute-start.23 = (bf16[256,512]{1,0:T(8,128)(2,1)}, bf16[256,512]{1,0:T(8,128)(2,1)S(1)}, u32[]{:S(2)}, u32[]{:S(2)}) collective-permute-start(bf16[256,512]{1,0:T(8,128)(2,1)} %get-tuple-element.75), channel_id=1, source_target_pairs={{0,16},{8,24},{16,0},{24,8},{1,17},{9,25},{17,1},{25,9},{2,18},{10... | collective-permute-start | bytes 786440 | tf_op jit(solution)/shard_map/ppermute | solution.py:120
  93.6 7.6 %collective-permute-done.24.refs_3_ = bf16[256,512]{1,0:T(8,128)(2,1)S(1)} collective-permute-done((bf16[256,512]{1,0:T(8,128)(2,1)}, bf16[256,512]{1,0:T(8,128)(2,1)S(1)}, u32[]{:S(2)}, u32[]{:S(2)}) %collective-permute-start.24) | collective-permute-done | bytes 262176 | tf_op jit(solution)/shard_map/ppermute | solution.py:120
  102.0 2.8 %collective-permute-start.26 = (bf16[256,512]{1,0:T(8,128)(2,1)S(1)}, bf16[256,512]{1,0:T(8,128)(2,1)S(1)}, u32[]{:S(2)}, u32[]{:S(2)}) collective-permute-start(bf16[256,512]{1,0:T(8,128)(2,1)S(1)} %get-tuple-element.79), channel_id=1, source_target_pairs={{0,64},{32,96},{64,0},{96,32},{1,65},{33,97},{65,1},{97,33},{2,66}... | collective-permute-start | bytes 786440 | tf_op jit(solution)/shard_map/ppermute | solution.py:120
  111.2 8.4 %collective-permute-done.27.refs_4_ = bf16[256,512]{1,0:T(8,128)(2,1)S(1)} collective-permute-done((bf16[256,512]{1,0:T(8,128)(2,1)S(1)}, bf16[256,512]{1,0:T(8,128)(2,1)S(1)}, u32[]{:S(2)}, u32[]{:S(2)}) %collective-permute-start.27) | collective-permute-done | bytes 262176 | tf_op jit(solution)/shard_map/ppermute | solution.py:120
  123.1 2.2 %collective-permute-done.15.refs_4_ = bf16[256,512]{1,0:T(8,128)(2,1)} collective-permute-done((bf16[256,512]{1,0:T(8,128)(2,1)S(1)}, bf16[256,512]{1,0:T(8,128)(2,1)}, u32[]{:S(2)}, u32[]{:S(2)}) %collective-permute-start.15) | collective-permute-done | bytes 262176 | tf_op jit(solution)/shard_map/ppermute | solution.py:120
  125.3 2.7 %shard_map.31 = (bf16[256,512]{1,0:T(8,128)(2,1)S(1)}, bf16[256,512]{1,0:T(8,128)(2,1)S(1)}, bf16[256,512]{1,0:T(8,128)(2,1)S(1)}, bf16[256,512]{1,0:T(8,128)(2,1)S(1)}) custom-call(s32[10]{0:T(128)S(1)} %pad_add_fusion.order, bf16[4,4,256,256]{3,2,1,0:T(8,128)(2,1)S(1)} %copy-done.3, bf16[256,512]{1,0:T(8,128)(2,1)S(1)} %get-tuple-element.61.refs_1_, ...), custom_call_target="tpu_custom_call" | custom-call | flops 1073741824 | bytes 4194304 | tf_op jit(solution)/shard_map/pallas_call | solution.py:52
  130.7 3.8 %collective-permute-start.17 = (bf16[256,512]{1,0:T(8,128)(2,1)S(1)}, bf16[256,512]{1,0:T(8,128)(2,1)S(1)}, u32[]{:S(2)}, u32[]{:S(2)}) collective-permute-start(bf16[256,512]{1,0:T(8,128)(2,1)S(1)} %get-tuple-element.67), channel_id=1, source_target_pairs={{0,64},{32,96},{64,0},{96,32},{1,65},{33,97},{65,1},{97,33},{2,66}... | collective-permute-start | bytes 786440 | tf_op jit(solution)/shard_map/ppermute | solution.py:120
  134.7 5.9 %collective-permute-done.29.refs_2_ = bf16[256,512]{1,0:T(8,128)(2,1)S(1)} collective-permute-done((bf16[256,512]{1,0:T(8,128)(2,1)S(1)}, bf16[256,512]{1,0:T(8,128)(2,1)S(1)}, u32[]{:S(2)}, u32[]{:S(2)}) %collective-permute-start.29) | collective-permute-done | bytes 262176 | tf_op jit(solution)/shard_map/ppermute | solution.py:120
  140.5 6.0 %collective-permute-done.30.refs_3_ = bf16[256,512]{1,0:T(8,128)(2,1)S(1)} collective-permute-done((bf16[256,512]{1,0:T(8,128)(2,1)S(1)}, bf16[256,512]{1,0:T(8,128)(2,1)S(1)}, u32[]{:S(2)}, u32[]{:S(2)}) %collective-permute-start.30) | collective-permute-done | bytes 262176 | tf_op jit(solution)/shard_map/ppermute | solution.py:120
  148.7 3.1 %collective-permute-done.17.refs_2_ = bf16[256,512]{1,0:T(8,128)(2,1)S(1)} collective-permute-done((bf16[256,512]{1,0:T(8,128)(2,1)S(1)}, bf16[256,512]{1,0:T(8,128)(2,1)S(1)}, u32[]{:S(2)}, u32[]{:S(2)}) %collective-permute-start.17) | collective-permute-done | bytes 262176 | tf_op jit(solution)/shard_map/ppermute | solution.py:120
  151.8 2.8 %collective-permute-done.18.refs_3_ = bf16[256,512]{1,0:T(8,128)(2,1)S(1)} collective-permute-done((bf16[256,512]{1,0:T(8,128)(2,1)S(1)}, bf16[256,512]{1,0:T(8,128)(2,1)S(1)}, u32[]{:S(2)}, u32[]{:S(2)}) %collective-permute-start.18) | collective-permute-done | bytes 262176 | tf_op jit(solution)/shard_map/ppermute | solution.py:120
  154.6 2.1 %shard_map.37 = bf16[4,256,1024]{2,1,0:T(8,128)(2,1)} custom-call(s32[4]{0:T(128)S(1)} %and_select_fusion.5.order, bf16[256,512]{1,0:T(8,128)(2,1)S(1)} %get-tuple-element.65.refs_0_, bf16[256,512]{1,0:T(8,128)(2,1)S(1)} %collective-permute-done.16.refs_1_, bf16[256,512]{1,0:T(8,128)(2,1)S(1)} %collective-permute-done.17.refs_2_, ...), custom_call_target="tpu_custom_call", output_to_operand_aliasing={{}: (5, {})} | custom-call | tf_op jit(solution)/shard_map/pallas_call | solution.py:82
  (104 shorter events, 36.5 us)
Async XLA Ops:
  14.8 17.1 %collective-permute-start = (bf16[4,4,32,256]{3,2,1,0:T(8,128)(2,1)S(1)}, bf16[4,4,32,256]{3,2,1,0:T(8,128)(2,1)S(1)}, u32[]{:S(2)}, u32[]{:S(2)}) collective-permute-start(bf16[4,4,32,256]{3,2,1,0:T(8,128)(2,1)S(1)} %get-tuple-element.86.refs_0_), channel_id=1, source_target_pairs={{0,2},{2,4},{4,6},{6,0},{1,3},{3,5},{5,7},{7,1},{8,10},{10,12},{12... | collective-permute-start | bytes 786440 | tf_op jit(solution)/shard_map/ppermute | solution.py:120
  18.1 13.8 %collective-permute-start.1 = (bf16[4,4,32,256]{3,2,1,0:T(8,128)(2,1)S(1)}, bf16[4,4,32,256]{3,2,1,0:T(8,128)(2,1)S(1)}, u32[]{:S(2)}, u32[]{:S(2)}) collective-permute-start(bf16[4,4,32,256]{3,2,1,0:T(8,128)(2,1)S(1)} %get-tuple-element.86.refs_0_), channel_id=1, source_target_pairs={{0,6},{2,0},{4,2},{6,4},{1,7},{3,1},{5,3},{7,5},{8,14},{10,8},{12,... | collective-permute-start | bytes 786440 | tf_op jit(solution)/shard_map/ppermute | solution.py:120
  20.2 11.7 %all-to-all-start.1 = ((bf16[4,4,32,256]{3,2,1,0:T(8,128)(2,1)}), bf16[4,4,32,256]{3,2,1,0:T(8,128)(2,1)S(1)}, u32[]{:S(2)}, u32[]{:S(2)}) async-start(bf16[4,4,32,256]{3,2,1,0:T(8,128)(2,1)} %get-tuple-element.46), calls=%async_computation.1 | async-start | bytes 524288 | tf_op jit(solution)/shard_map/all_to_all | solution.py:148
  24.9 49.2 %all-gather.5.cloned.1.call-start = ((), (), s32[]{:S(2)}) async-start(), calls=%async_computation.3 | async-start | bytes 2359296 | tf_op jit(solution)/shard_map/all_gather | solution.py:152
  31.9 79.2 %all-gather.3.cloned.1.call-start = ((), (), s32[]{:S(2)}) async-start(), calls=%async_computation.2 | async-start | bytes 2359296 | tf_op jit(solution)/shard_map/all_gather | solution.py:152
  32.0 16.9 %collective-permute-start.5 = (bf16[4,4,32,256]{3,2,1,0:T(8,128)(2,1)S(1)}, bf16[4,4,32,256]{3,2,1,0:T(8,128)(2,1)S(1)}, u32[]{:S(2)}, u32[]{:S(2)}) collective-permute-start(bf16[4,4,32,256]{3,2,1,0:T(8,128)(2,1)S(1)} %get-tuple-element.86.refs_0_), channel_id=1, source_target_pairs={{0,4},{2,6},{4,0},{6,2},{1,5},{3,7},{5,1},{7,3},{8,12},{10,14},{12... | collective-permute-start | bytes 786440 | tf_op jit(solution)/shard_map/ppermute | solution.py:120
  59.5 14.6 %collective-permute-start.21 = (bf16[256,512]{1,0:T(8,128)(2,1)}, bf16[256,512]{1,0:T(8,128)(2,1)S(1)}, u32[]{:S(2)}, u32[]{:S(2)}) collective-permute-start(bf16[256,512]{1,0:T(8,128)(2,1)} %get-tuple-element.72), channel_id=1, source_target_pairs={{0,24},{8,0},{16,8},{24,16},{1,25},{9,1},{17,9},{25,17},{2,26},{10... | collective-permute-start | bytes 786440 | tf_op jit(solution)/shard_map/ppermute | solution.py:120
  64.1 20.8 %collective-permute-start.7 = (bf16[256,512]{1,0:T(8,128)(2,1)}, bf16[256,512]{1,0:T(8,128)(2,1)S(1)}, u32[]{:S(2)}, u32[]{:S(2)}) collective-permute-start(bf16[256,512]{1,0:T(8,128)(2,1)} %get-tuple-element.54), channel_id=1, source_target_pairs={{0,8},{8,16},{16,24},{24,0},{1,9},{9,17},{17,25},{25,1},{2,10},{10... | collective-permute-start | bytes 786440 | tf_op jit(solution)/shard_map/ppermute | solution.py:120
  67.5 18.8 %collective-permute-start.8 = (bf16[256,512]{1,0:T(8,128)(2,1)}, bf16[256,512]{1,0:T(8,128)(2,1)S(1)}, u32[]{:S(2)}, u32[]{:S(2)}) collective-permute-start(bf16[256,512]{1,0:T(8,128)(2,1)} %get-tuple-element.55), channel_id=1, source_target_pairs={{0,16},{8,24},{16,0},{24,8},{1,17},{9,25},{17,1},{25,9},{2,18},{10... | collective-permute-start | bytes 786440 | tf_op jit(solution)/shard_map/ppermute | solution.py:120
  67.7 18.5 %collective-permute-start.9 = (bf16[256,512]{1,0:T(8,128)(2,1)}, bf16[256,512]{1,0:T(8,128)(2,1)S(1)}, u32[]{:S(2)}, u32[]{:S(2)}) collective-permute-start(bf16[256,512]{1,0:T(8,128)(2,1)} %get-tuple-element.56), channel_id=1, source_target_pairs={{0,24},{8,0},{16,8},{24,16},{1,25},{9,1},{17,9},{25,17},{2,26},{10... | collective-permute-start | bytes 786440 | tf_op jit(solution)/shard_map/ppermute | solution.py:120
  79.3 12.5 %collective-permute-start.22 = (bf16[256,512]{1,0:T(8,128)(2,1)}, bf16[256,512]{1,0:T(8,128)(2,1)S(1)}, u32[]{:S(2)}, u32[]{:S(2)}) collective-permute-start(bf16[256,512]{1,0:T(8,128)(2,1)} %get-tuple-element.74), channel_id=1, source_target_pairs={{0,8},{8,16},{16,24},{24,0},{1,9},{9,17},{17,25},{25,1},{2,10},{10... | collective-permute-start | bytes 786440 | tf_op jit(solution)/shard_map/ppermute | solution.py:120
  79.8 13.9 %collective-permute-start.23 = (bf16[256,512]{1,0:T(8,128)(2,1)}, bf16[256,512]{1,0:T(8,128)(2,1)S(1)}, u32[]{:S(2)}, u32[]{:S(2)}) collective-permute-start(bf16[256,512]{1,0:T(8,128)(2,1)} %get-tuple-element.75), channel_id=1, source_target_pairs={{0,16},{8,24},{16,0},{24,8},{1,17},{9,25},{17,1},{25,9},{2,18},{10... | collective-permute-start | bytes 786440 | tf_op jit(solution)/shard_map/ppermute | solution.py:120
  84.9 16.3 %collective-permute-start.24 = (bf16[256,512]{1,0:T(8,128)(2,1)}, bf16[256,512]{1,0:T(8,128)(2,1)S(1)}, u32[]{:S(2)}, u32[]{:S(2)}) collective-permute-start(bf16[256,512]{1,0:T(8,128)(2,1)} %get-tuple-element.76), channel_id=1, source_target_pairs={{0,24},{8,0},{16,8},{24,16},{1,25},{9,1},{17,9},{25,17},{2,26},{10... | collective-permute-start | bytes 786440 | tf_op jit(solution)/shard_map/ppermute | solution.py:120
  89.6 15.2 %collective-permute-start.10 = (bf16[256,512]{1,0:T(8,128)(2,1)S(1)}, bf16[256,512]{1,0:T(8,128)(2,1)S(1)}, u32[]{:S(2)}, u32[]{:S(2)}) collective-permute-start(bf16[256,512]{1,0:T(8,128)(2,1)S(1)} %get-tuple-element.58), channel_id=1, source_target_pairs={{0,8},{8,16},{16,24},{24,0},{1,9},{9,17},{17,25},{25,1},{2,10},{10... | collective-permute-start | bytes 786440 | tf_op jit(solution)/shard_map/ppermute | solution.py:120
  91.6 13.3 %collective-permute-start.11 = (bf16[256,512]{1,0:T(8,128)(2,1)S(1)}, bf16[256,512]{1,0:T(8,128)(2,1)S(1)}, u32[]{:S(2)}, u32[]{:S(2)}) collective-permute-start(bf16[256,512]{1,0:T(8,128)(2,1)S(1)} %get-tuple-element.59), channel_id=1, source_target_pairs={{0,16},{8,24},{16,0},{24,8},{1,17},{9,25},{17,1},{25,9},{2,18},{10... | collective-permute-start | bytes 786440 | tf_op jit(solution)/shard_map/ppermute | solution.py:120
  91.8 14.8 %collective-permute-start.12 = (bf16[256,512]{1,0:T(8,128)(2,1)S(1)}, bf16[256,512]{1,0:T(8,128)(2,1)S(1)}, u32[]{:S(2)}, u32[]{:S(2)}) collective-permute-start(bf16[256,512]{1,0:T(8,128)(2,1)S(1)} %get-tuple-element.60), channel_id=1, source_target_pairs={{0,24},{8,0},{16,8},{24,16},{1,25},{9,1},{17,9},{25,17},{2,26},{10... | collective-permute-start | bytes 786440 | tf_op jit(solution)/shard_map/ppermute | solution.py:120
  104.8 14.8 %collective-permute-start.27 = (bf16[256,512]{1,0:T(8,128)(2,1)S(1)}, bf16[256,512]{1,0:T(8,128)(2,1)S(1)}, u32[]{:S(2)}, u32[]{:S(2)}) collective-permute-start(bf16[256,512]{1,0:T(8,128)(2,1)S(1)} %get-tuple-element.80), channel_id=1, source_target_pairs={{0,96},{32,0},{64,32},{96,64},{1,97},{33,1},{65,33},{97,65},{2,98}... | collective-permute-start | bytes 786440 | tf_op jit(solution)/shard_map/ppermute | solution.py:120
  108.0 15.1 %collective-permute-start.13 = (bf16[256,512]{1,0:T(8,128)(2,1)}, bf16[256,512]{1,0:T(8,128)(2,1)S(1)}, u32[]{:S(2)}, u32[]{:S(2)}) collective-permute-start(bf16[256,512]{1,0:T(8,128)(2,1)} %get-tuple-element.62), channel_id=1, source_target_pairs={{0,32},{32,64},{64,96},{96,0},{1,33},{33,65},{65,97},{97,1},{2,34}... | collective-permute-start | bytes 786440 | tf_op jit(solution)/shard_map/ppermute | solution.py:120
  109.8 13.3 %collective-permute-start.14 = (bf16[256,512]{1,0:T(8,128)(2,1)S(1)}, bf16[256,512]{1,0:T(8,128)(2,1)S(1)}, u32[]{:S(2)}, u32[]{:S(2)}) collective-permute-start(bf16[256,512]{1,0:T(8,128)(2,1)S(1)} %get-tuple-element.63), channel_id=1, source_target_pairs={{0,64},{32,96},{64,0},{96,32},{1,65},{33,97},{65,1},{97,33},{2,66}... | collective-permute-start | bytes 786440 | tf_op jit(solution)/shard_map/ppermute | solution.py:120
  110.8 14.5 %collective-permute-start.15 = (bf16[256,512]{1,0:T(8,128)(2,1)S(1)}, bf16[256,512]{1,0:T(8,128)(2,1)}, u32[]{:S(2)}, u32[]{:S(2)}) collective-permute-start(bf16[256,512]{1,0:T(8,128)(2,1)S(1)} %get-tuple-element.64), channel_id=1, source_target_pairs={{0,96},{32,0},{64,32},{96,64},{1,97},{33,1},{65,33},{97,65},{2,98}... | collective-permute-start | bytes 786440 | tf_op jit(solution)/shard_map/ppermute | solution.py:120
  128.0 20.6 %collective-permute-start.16 = (bf16[256,512]{1,0:T(8,128)(2,1)S(1)}, bf16[256,512]{1,0:T(8,128)(2,1)S(1)}, u32[]{:S(2)}, u32[]{:S(2)}) collective-permute-start(bf16[256,512]{1,0:T(8,128)(2,1)S(1)} %get-tuple-element.66), channel_id=1, source_target_pairs={{0,32},{32,64},{64,96},{96,0},{1,33},{33,65},{65,97},{97,1},{2,34}... | collective-permute-start | bytes 786440 | tf_op jit(solution)/shard_map/ppermute | solution.py:120
  130.6 16.0 %collective-permute-start.30 = (bf16[256,512]{1,0:T(8,128)(2,1)S(1)}, bf16[256,512]{1,0:T(8,128)(2,1)S(1)}, u32[]{:S(2)}, u32[]{:S(2)}) collective-permute-start(bf16[256,512]{1,0:T(8,128)(2,1)S(1)} %get-tuple-element.84), channel_id=1, source_target_pairs={{0,96},{32,0},{64,32},{96,64},{1,97},{33,1},{65,33},{97,65},{2,98}... | collective-permute-start | bytes 786440 | tf_op jit(solution)/shard_map/ppermute | solution.py:120
  130.7 21.0 %collective-permute-start.17 = (bf16[256,512]{1,0:T(8,128)(2,1)S(1)}, bf16[256,512]{1,0:T(8,128)(2,1)S(1)}, u32[]{:S(2)}, u32[]{:S(2)}) collective-permute-start(bf16[256,512]{1,0:T(8,128)(2,1)S(1)} %get-tuple-element.67), channel_id=1, source_target_pairs={{0,64},{32,96},{64,0},{96,32},{1,65},{33,97},{65,1},{97,33},{2,66}... | collective-permute-start | bytes 786440 | tf_op jit(solution)/shard_map/ppermute | solution.py:120
  134.5 20.1 %collective-permute-start.18 = (bf16[256,512]{1,0:T(8,128)(2,1)S(1)}, bf16[256,512]{1,0:T(8,128)(2,1)S(1)}, u32[]{:S(2)}, u32[]{:S(2)}) collective-permute-start(bf16[256,512]{1,0:T(8,128)(2,1)S(1)} %get-tuple-element.68), channel_id=1, source_target_pairs={{0,96},{32,0},{64,32},{96,64},{1,97},{33,1},{65,33},{97,65},{2,98}... | collective-permute-start | bytes 786440 | tf_op jit(solution)/shard_map/ppermute | solution.py:120
  (30 other events, 328.1 us)
Sparse Core Ops, SparseCore 0:
  32.1 38.6 all-gather.4
  72.6 34.0 all-gather.2

commit v3 on v2

--- a/solution.py
+++ b/solution.py
@@ -144,12 +144,13 @@
     return [blocks[0]] + [shift(blocks[s], axis, s) for s in (1, 2, 3)]
 
 
-def hand_over(shard, axis):
-    return lax.all_to_all(shard, axis, 0, 0, tiled=True)
+def hand_over(shards):
+    first, second = lax.all_to_all(shards, "y", 1, 1, tiled=True)
+    return jnp.stack([lax.all_to_all(first, "x", 0, 0, tiled=True), second])
 
 
 def all_rows(mine):
-    return lax.all_gather(mine, ("zh", "core"), axis=2, tiled=True)
+    return lax.all_gather(mine, ("zh", "core"), axis=3, tiled=True)
 
 
 def local(coefficients, transfer):
@@ -161,29 +162,24 @@
         head = jnp.stack([core, zh])
         return jnp.concatenate([head, slots % 4, children % 4]).astype(jnp.int32)
 
-    order0 = order(a + steps, steps)
+    order0 = order(b + steps, steps)
+    orders = ((b - a - steps + 8) % 4).astype(jnp.int32)
     order1 = order(a + steps, a - steps + 4)
-    order2 = order(b + steps, b - steps + 4)
-    orders = ((a - b - steps + 8) % 4).astype(jnp.int32)
+    order2 = order(b + steps, a - steps + 4)
     orderp = ((b - steps + 4) % 4).astype(jnp.int32)
 
     pieces = z_pieces(transfer[0])
     first = swap(pieces[0])
-    mine1 = hand_over(after(transfer[1], first), "x")
-    mine2 = hand_over(after(transfer[2], mine1), "y")
-    *near, mine1, mine2 = lax.optimization_barrier((*pieces[1:3], mine1, mine2))
-    w0 = [pieces[0], first] + both_cores(near + pieces[3:])
-    w1 = all_rows(after(mine1, *near))
-    w2 = all_rows(after(mine2, *w0))
-    states = [
-        exchange(level(order0, w0, [coefficients], PIECES, c, ALL_VMEM), "x") for c in range(CHUNKS)
-    ]
+    mine = hand_over(transfer[1:])
+    w0 = [pieces[0], first] + both_cores(pieces[1:])
+    w1, w2 = all_rows(after(mine, *w0))
+    states = []
     for c in range(CHUNKS):
-        memory = VMEM if c else ALL_VMEM
-        states[c] = exchange(level(order1, [w1], states[c], vmem=memory), "x")
-        states[c] = exchange(select(orders, states[c]), "y")
-    for c in range(CHUNKS):
-        states[c] = exchange(level(order2, [w2], states[c]), "y")
+        blocks = exchange(level(order0, w0, [coefficients], PIECES, c, ALL_VMEM), "y")
+        states.append(blocks)
+    states = [exchange(select(orders, blocks), "x") for blocks in states]
+    states = [exchange(level(order1, [w1], blocks), "x") for blocks in states]
+    states = [exchange(level(order2, [w2], blocks), "y") for blocks in states]
     result = None
     for c in range(CHUNKS):
         result = place(orderp, states[c], c, result)

time: 166 us -> 162 us (0.976)
  starting transfers between devices: 50.2 us -> 45.5 us
  Pallas kernels: 26.3 us -> 22.9 us
  waiting for transfers between devices: 66.7 us -> 69.5 us
    all_gather x2 -> x1, waiting for transfers between devices: 0.01 us -> 16.3 us  [all_rows(): return lax.all_gather(mine, ('zh', 'core'), axis=3, tiled=True)]
    ppermute x31, waiting for transfers between devices: 66.7 us -> 53.2 us  [shift(): lax.ppermute(array, axis, [(i, (i + by) % size) for i in range(size)])]
    ppermute x31, starting transfers between devices: 40.7 us -> 36.1 us  [shift(): lax.ppermute(array, axis, [(i, (i + by) % size) for i in range(size)])]
    pallas_call x6, Pallas kernels: 19.9 us -> 16.5 us  [level(): pl.pallas_call(functools.partial(level_kernel, pieces), grid_spec=pltpu.P...]
    another operation x0 -> x2, local copies, waits for them, and re-layouts: none -> 3.4 us  [the longest x1 2.65 us: local(): w1, w2 = all_rows(after(mine, *w0))]
    unnamed x38 -> x21, local copies, waits for them, and re-layouts: 3.98 us -> 1.83 us
  transfers between devices with their start and end apart: 35 -> 34, of which waited for: 16 -> 15; matrix products, arithmetic and copies ran while one was open for 0% -> 4% of each run, Pallas kernels for 15% -> 13%
where the time goes in v3:
time: 162 us; the launch traced here: 160 us
  waiting for transfers between devices  69.5 us (43%)
  starting transfers between devices  45.5 us (28%)
  Pallas kernels  22.9 us (14%)
  between operations  13.6 us (8%)
  local copies, waits for them, and re-layouts  7.28 us (4%)
    ppermute x31, waiting for transfers between devices, shift(): lax.ppermute(array, axis, [(i, (i + by) % size) for i in range(size)])  53.2 us
    ppermute x31, starting transfers between devices, shift(): lax.ppermute(array, axis, [(i, (i + by) % size) for i in range(size)])  36.1 us
    pallas_call x6, Pallas kernels, level(): pl.pallas_call(functools.partial(level_kernel, pieces), grid_spec=pltpu.P...  16.5 us
    all_gather x1, waiting for transfers between devices, all_rows(): return lax.all_gather(mine, ('zh', 'core'), axis=3, tiled=True)  16.3 us
    all_to_all x1, starting transfers between devices, hand_over(): return jnp.stack([lax.all_to_all(first, 'x', 0, 0, tiled=True), second])  4.77 us
    all_to_all x1, starting transfers between devices, hand_over(): first, second = lax.all_to_all(shards, 'y', 1, 1, tiled=True)  4.68 us
    pallas_call x2, Pallas kernels, place(): pl.pallas_call(place_kernel, grid_spec=pltpu.PrefetchScalarGridSpec(num_s...  4.23 us
  transfers between devices with their start and end apart: 34, of which 15 were waited for; matrix products, arithmetic and copies ran while one was open for 4% of the time, Pallas kernels for 13%

profile of v3, /device:TPU:62, one launch (start us, length us, event | category | flops | bytes accessed | tf_op | source)
XLA Modules:
  0.0 160.4 jit_solution(3537790301158731393)
XLA Ops:
  8.5 4.7 %all-to-all-start = ((bf16[2,4,4,32,256]{4,3,2,0,1:T(8,128)(2,1)}), bf16[2,4,4,32,256]{4,3,2,0,1:T(8,128)(2,1)S(1)}, u32[]{:S(2)}, u32[]{:S(2)}) async-start(bf16[2,4,4,32,256]{4,3,2,0,1:T(8,128)(2,1)} %copy.7), calls=%async_computation | async-start | bytes 1048576 | tf_op jit(solution)/shard_map/all_to_all | solution.py:148
  14.1 6.4 %collective-permute-start.5 = (bf16[4,4,32,256]{3,2,1,0:T(8,128)(2,1)S(1)}, bf16[4,4,32,256]{3,2,1,0:T(8,128)(2,1)S(1)}, u32[]{:S(2)}, u32[]{:S(2)}) collective-permute-start(bf16[4,4,32,256]{3,2,1,0:T(8,128)(2,1)S(1)} %slice_bitcast_fusion.4.refs_0_), channel_id=1, source_target_pairs={{0,4},{2,6},{4,0},{6,2},{1,5},{3,7},{5,1},{7,3},{8,12},{10,14},{12... | collective-permute-start | bytes 786440 | tf_op jit(solution)/shard_map/ppermute | solution.py:120
  21.1 2.4 %collective-permute-start.1 = (bf16[4,4,32,256]{3,2,1,0:T(8,128)(2,1)S(1)}, bf16[4,4,32,256]{3,2,1,0:T(8,128)(2,1)S(1)}, u32[]{:S(2)}, u32[]{:S(2)}) collective-permute-start(bf16[4,4,32,256]{3,2,1,0:T(8,128)(2,1)S(1)} %slice_bitcast_fusion.4.refs_0_), channel_id=1, source_target_pairs={{0,2},{2,4},{4,6},{6,0},{1,3},{3,5},{5,7},{7,1},{8,10},{10,12},{12... | collective-permute-start | bytes 786440 | tf_op jit(solution)/shard_map/ppermute | solution.py:120
  24.2 4.8 %all-to-all-start.1 = ((bf16[4,4,32,256]{3,2,1,0:T(8,128)(2,1)}), bf16[4,4,32,256]{3,2,1,0:T(8,128)(2,1)S(1)}, u32[]{:S(2)}, u32[]{:S(2)}) async-start(bf16[4,4,32,256]{3,2,1,0:T(8,128)(2,1)} %get-tuple-element.73), calls=%async_computation.1 | async-start | bytes 524288 | tf_op jit(solution)/shard_map/all_to_all | solution.py:149
  29.0 5.8 %collective-permute-done.5.refs_6_ = bf16[4,4,32,256]{3,2,1,0:T(8,128)(2,1)S(1)} collective-permute-done((bf16[4,4,32,256]{3,2,1,0:T(8,128)(2,1)S(1)}, bf16[4,4,32,256]{3,2,1,0:T(8,128)(2,1)S(1)}, u32[]{:S(2)}, u32[]{:S(2)}) %collective-permute-start.5) | collective-permute-done | bytes 262176 | tf_op jit(solution)/shard_map/ppermute | solution.py:120
  34.7 7.7 %collective-permute-done.3.refs_4_ = bf16[4,4,32,256]{3,2,1,0:T(8,128)(2,1)S(1)} collective-permute-done((bf16[4,4,32,256]{3,2,1,0:T(8,128)(2,1)S(1)}, bf16[4,4,32,256]{3,2,1,0:T(8,128)(2,1)S(1)}, u32[]{:S(2)}, u32[]{:S(2)}) %collective-permute-start.3) | collective-permute-done | bytes 262176 | tf_op jit(solution)/shard_map/ppermute | solution.py:120
  45.3 4.6 %shard_map.32 = (bf16[256,512]{1,0:T(8,128)(2,1)}, bf16[256,512]{1,0:T(8,128)(2,1)}, bf16[256,512]{1,0:T(8,128)(2,1)}, bf16[256,512]{1,0:T(8,128)(2,1)}) custom-call(s32[10]{0:T(128)} %get-tuple-element.75.order, bf16[4,4,32,256]{3,2,1,0:T(8,128)(2,1)} %copy-done.2, bf16[4,4,32,256]{3,2,1,0:T(8,128)(2,1)} %copy-done.6, bf16[4,4,32,256]{3,2,1,0:T(8,128)(2,1)} %copy-done.5, ...), custom_call_target="tpu_custom_call" | custom-call | flops 1073741824 | bytes 4194304 | tf_op jit(solution)/shard_map/pallas_call | solution.py:52
  50.3 2.6 %collective-permute-start.20 = (bf16[256,512]{1,0:T(8,128)(2,1)}, bf16[256,512]{1,0:T(8,128)(2,1)S(1)}, u32[]{:S(2)}, u32[]{:S(2)}) collective-permute-start(bf16[256,512]{1,0:T(8,128)(2,1)} %get-tuple-element.57), channel_id=1, source_target_pairs={{0,64},{32,96},{64,0},{96,32},{1,65},{33,97},{65,1},{97,33},{2,66}... | collective-permute-start | bytes 786440 | tf_op jit(solution)/shard_map/ppermute | solution.py:120
  52.9 4.8 %shard_map.28 = (bf16[256,512]{1,0:T(8,128)(2,1)}, bf16[256,512]{1,0:T(8,128)(2,1)}, bf16[256,512]{1,0:T(8,128)(2,1)}, bf16[256,512]{1,0:T(8,128)(2,1)}) custom-call(s32[10]{0:T(128)} %get-tuple-element.75.order, bf16[4,4,32,256]{3,2,1,0:T(8,128)(2,1)} %copy-done.2, bf16[4,4,32,256]{3,2,1,0:T(8,128)(2,1)} %copy-done.6, bf16[4,4,32,256]{3,2,1,0:T(8,128)(2,1)} %copy-done.5, ...), custom_call_target="tpu_custom_call" | custom-call | flops 1073741824 | bytes 4194304 | tf_op jit(solution)/shard_map/pallas_call | solution.py:52
  57.7 3.3 %collective-permute-start.7 = (bf16[256,512]{1,0:T(8,128)(2,1)}, bf16[256,512]{1,0:T(8,128)(2,1)S(1)}, u32[]{:S(2)}, u32[]{:S(2)}) collective-permute-start(bf16[256,512]{1,0:T(8,128)(2,1)} %get-tuple-element.40), channel_id=1, source_target_pairs={{0,32},{32,64},{64,96},{96,0},{1,33},{33,65},{65,97},{97,1},{2,34}... | collective-permute-start | bytes 786440 | tf_op jit(solution)/shard_map/ppermute | solution.py:120
  62.3 4.6 %collective-permute-done.21.refs_3_ = bf16[256,512]{1,0:T(8,128)(2,1)S(1)} collective-permute-done((bf16[256,512]{1,0:T(8,128)(2,1)}, bf16[256,512]{1,0:T(8,128)(2,1)S(1)}, u32[]{:S(2)}, u32[]{:S(2)}) %collective-permute-start.21) | collective-permute-done | bytes 262176 | tf_op jit(solution)/shard_map/ppermute | solution.py:120
  68.2 2.4 %collective-permute-start.23 = (bf16[256,512]{1,0:T(8,128)(2,1)S(1)}, bf16[256,512]{1,0:T(8,128)(2,1)S(1)}, u32[]{:S(2)}, u32[]{:S(2)}) collective-permute-start(bf16[256,512]{1,0:T(8,128)(2,1)S(1)} %get-tuple-element.61), channel_id=1, source_target_pairs={{0,16},{8,24},{16,0},{24,8},{1,17},{9,25},{17,1},{25,9},{2,18},{10... | collective-permute-start | bytes 786440 | tf_op jit(solution)/shard_map/ppermute | solution.py:120
  72.5 4.4 %collective-permute-done.9.refs_3_ = bf16[256,512]{1,0:T(8,128)(2,1)S(1)} collective-permute-done((bf16[256,512]{1,0:T(8,128)(2,1)}, bf16[256,512]{1,0:T(8,128)(2,1)S(1)}, u32[]{:S(2)}, u32[]{:S(2)}) %collective-permute-start.9) | collective-permute-done | bytes 262176 | tf_op jit(solution)/shard_map/ppermute | solution.py:120
  79.8 2.4 %collective-permute-start.11 = (bf16[256,512]{1,0:T(8,128)(2,1)S(1)}, bf16[256,512]{1,0:T(8,128)(2,1)S(1)}, u32[]{:S(2)}, u32[]{:S(2)}) collective-permute-start(bf16[256,512]{1,0:T(8,128)(2,1)S(1)} %get-tuple-element.45), channel_id=1, source_target_pairs={{0,16},{8,24},{16,0},{24,8},{1,17},{9,25},{17,1},{25,9},{2,18},{10... | collective-permute-start | bytes 786440 | tf_op jit(solution)/shard_map/ppermute | solution.py:120
  82.2 16.3 %all-gather.2.cloned.1.call-done = bf16[2,4,4,256,256]{4,3,2,1,0:T(8,128)(2,1)} async-done(((bf16[2,4,4,32,256]{4,3,2,1,0:T(8,128)(2,1)}), bf16[2,4,4,256,256]{4,3,2,1,0:T(8,128)(2,1)}) %all-gather.2.cloned.1.call-update) | async-done | bytes 4194320 | tf_op jit(solution)/shard_map/all_gather | solution.py:153
  98.5 2.6 %slice_bitcast_fusion = (bf16[4,4,256,256]{3,2,1,0:T(8,128)(2,1)S(1)}, bf16[4,4,256,256]{3,2,1,0:T(8,128)(2,1)S(1)}) fusion(bf16[2,4,4,256,256]{4,3,2,1,0:T(8,128)(2,1)} %all-gather.2.cloned.1.call-done), kind=kLoop, calls=%fused_computation | loop fusion | bytes 8388608 | tf_op jit(solution)/shard_map/unstack | solution.py:175
  103.8 2.5 %collective-permute-start.25 = (bf16[256,512]{1,0:T(8,128)(2,1)S(1)}, bf16[256,512]{1,0:T(8,128)(2,1)S(1)}, u32[]{:S(2)}, u32[]{:S(2)}) collective-permute-start(bf16[256,512]{1,0:T(8,128)(2,1)S(1)} %get-tuple-element.64), channel_id=1, source_target_pairs={{0,8},{8,16},{16,24},{24,0},{1,9},{9,17},{17,25},{25,1},{2,10},{10... | collective-permute-start | bytes 786440 | tf_op jit(solution)/shard_map/ppermute | solution.py:120
  107.3 9.9 %collective-permute-done.12.refs_4_ = bf16[256,512]{1,0:T(8,128)(2,1)S(1)} collective-permute-done((bf16[256,512]{1,0:T(8,128)(2,1)S(1)}, bf16[256,512]{1,0:T(8,128)(2,1)S(1)}, u32[]{:S(2)}, u32[]{:S(2)}) %collective-permute-start.12) | collective-permute-done | bytes 262176 | tf_op jit(solution)/shard_map/ppermute | solution.py:120
  121.1 5.8 %collective-permute-done.27.refs_4_ = bf16[256,512]{1,0:T(8,128)(2,1)S(1)} collective-permute-done((bf16[256,512]{1,0:T(8,128)(2,1)S(1)}, bf16[256,512]{1,0:T(8,128)(2,1)S(1)}, u32[]{:S(2)}, u32[]{:S(2)}) %collective-permute-start.27) | collective-permute-done | bytes 262176 | tf_op jit(solution)/shard_map/ppermute | solution.py:120
  129.2 2.5 %collective-permute-start.29 = (bf16[256,512]{1,0:T(8,128)(2,1)S(1)}, bf16[256,512]{1,0:T(8,128)(2,1)S(1)}, u32[]{:S(2)}, u32[]{:S(2)}) collective-permute-start(bf16[256,512]{1,0:T(8,128)(2,1)S(1)} %get-tuple-element.69), channel_id=1, source_target_pairs={{0,64},{32,96},{64,0},{96,32},{1,65},{33,97},{65,1},{97,33},{2,66}... | collective-permute-start | bytes 786440 | tf_op jit(solution)/shard_map/ppermute | solution.py:120
  138.3 6.1 %collective-permute-done.30.refs_3_ = bf16[256,512]{1,0:T(8,128)(2,1)S(1)} collective-permute-done((bf16[256,512]{1,0:T(8,128)(2,1)S(1)}, bf16[256,512]{1,0:T(8,128)(2,1)S(1)}, u32[]{:S(2)}, u32[]{:S(2)}) %collective-permute-start.30) | collective-permute-done | bytes 262176 | tf_op jit(solution)/shard_map/ppermute | solution.py:120
  144.4 2.1 %shard_map.36.refs_4_ = bf16[4,256,1024]{2,1,0:T(8,128)(2,1)} custom-call(s32[4]{0:T(128)S(1)} %and_select_fusion.5.order, bf16[256,512]{1,0:T(8,128)(2,1)S(1)} %get-tuple-element.67.refs_0_, bf16[256,512]{1,0:T(8,128)(2,1)S(1)} %collective-permute-done.28.refs_1_, bf16[256,512]{1,0:T(8,128)(2,1)S(1)} %collective-permute-done.29.refs_2_, ...), custom_call_target="tpu_custom_call" | custom-call | tf_op jit(solution)/shard_map/pallas_call | solution.py:82
  147.6 3.8 %collective-permute-done.18.refs_3_ = bf16[256,512]{1,0:T(8,128)(2,1)S(1)} collective-permute-done((bf16[256,512]{1,0:T(8,128)(2,1)S(1)}, bf16[256,512]{1,0:T(8,128)(2,1)S(1)}, u32[]{:S(2)}, u32[]{:S(2)}) %collective-permute-start.18) | collective-permute-done | bytes 262176 | tf_op jit(solution)/shard_map/ppermute | solution.py:120
  151.4 2.1 %shard_map.37 = bf16[4,256,1024]{2,1,0:T(8,128)(2,1)} custom-call(s32[4]{0:T(128)S(1)} %and_select_fusion.5.order, bf16[256,512]{1,0:T(8,128)(2,1)S(1)} %get-tuple-element.51.refs_0_, bf16[256,512]{1,0:T(8,128)(2,1)S(1)} %collective-permute-done.16.refs_1_, bf16[256,512]{1,0:T(8,128)(2,1)S(1)} %collective-permute-done.17.refs_2_, ...), custom_call_target="tpu_custom_call", output_to_operand_aliasing={{}: (5, {})} | custom-call | tf_op jit(solution)/shard_map/pallas_call | solution.py:82
  (86 shorter events, 32.0 us)
Async XLA Ops:
  8.5 15.0 %all-to-all-start = ((bf16[2,4,4,32,256]{4,3,2,0,1:T(8,128)(2,1)}), bf16[2,4,4,32,256]{4,3,2,0,1:T(8,128)(2,1)S(1)}, u32[]{:S(2)}, u32[]{:S(2)}) async-start(bf16[2,4,4,32,256]{4,3,2,0,1:T(8,128)(2,1)} %copy.7), calls=%async_computation | async-start | bytes 1048576 | tf_op jit(solution)/shard_map/all_to_all | solution.py:148
  14.1 20.6 %collective-permute-start.5 = (bf16[4,4,32,256]{3,2,1,0:T(8,128)(2,1)S(1)}, bf16[4,4,32,256]{3,2,1,0:T(8,128)(2,1)S(1)}, u32[]{:S(2)}, u32[]{:S(2)}) collective-permute-start(bf16[4,4,32,256]{3,2,1,0:T(8,128)(2,1)S(1)} %slice_bitcast_fusion.4.refs_0_), channel_id=1, source_target_pairs={{0,4},{2,6},{4,0},{6,2},{1,5},{3,7},{5,1},{7,3},{8,12},{10,14},{12... | collective-permute-start | bytes 786440 | tf_op jit(solution)/shard_map/ppermute | solution.py:120
  20.5 21.9 %collective-permute-start.3 = (bf16[4,4,32,256]{3,2,1,0:T(8,128)(2,1)S(1)}, bf16[4,4,32,256]{3,2,1,0:T(8,128)(2,1)S(1)}, u32[]{:S(2)}, u32[]{:S(2)}) collective-permute-start(bf16[4,4,32,256]{3,2,1,0:T(8,128)(2,1)S(1)} %slice_bitcast_fusion.4.refs_0_), channel_id=1, source_target_pairs={{0,6},{2,0},{4,2},{6,4},{1,7},{3,1},{5,3},{7,5},{8,14},{10,8},{12,... | collective-permute-start | bytes 786440 | tf_op jit(solution)/shard_map/ppermute | solution.py:120
  21.1 22.0 %collective-permute-start.1 = (bf16[4,4,32,256]{3,2,1,0:T(8,128)(2,1)S(1)}, bf16[4,4,32,256]{3,2,1,0:T(8,128)(2,1)S(1)}, u32[]{:S(2)}, u32[]{:S(2)}) collective-permute-start(bf16[4,4,32,256]{3,2,1,0:T(8,128)(2,1)S(1)} %slice_bitcast_fusion.4.refs_0_), channel_id=1, source_target_pairs={{0,2},{2,4},{4,6},{6,0},{1,3},{3,5},{5,7},{7,1},{8,10},{10,12},{12... | collective-permute-start | bytes 786440 | tf_op jit(solution)/shard_map/ppermute | solution.py:120
  24.2 18.8 %all-to-all-start.1 = ((bf16[4,4,32,256]{3,2,1,0:T(8,128)(2,1)}), bf16[4,4,32,256]{3,2,1,0:T(8,128)(2,1)S(1)}, u32[]{:S(2)}, u32[]{:S(2)}) async-start(bf16[4,4,32,256]{3,2,1,0:T(8,128)(2,1)} %get-tuple-element.73), calls=%async_computation.1 | async-start | bytes 524288 | tf_op jit(solution)/shard_map/all_to_all | solution.py:149
  29.0 69.5 %all-gather.2.cloned.1.call-start = ((), (), s32[]{:S(2)}) async-start(), calls=%async_computation.2 | async-start | bytes 4718592 | tf_op jit(solution)/shard_map/all_gather | solution.py:153
  29.0 14.9 %collective-permute-start = (bf16[4,4,32,256]{3,2,1,0:T(8,128)(2,1)S(1)}, bf16[4,4,32,256]{3,2,1,0:T(8,128)(2,1)S(1)}, u32[]{:S(2)}, u32[]{:S(2)}) collective-permute-start(bf16[4,4,32,256]{3,2,1,0:T(8,128)(2,1)S(1)} %slice_bitcast_fusion.4.refs_0_), channel_id=1, source_target_pairs={{0,1},{1,0},{2,3},{3,2},{4,5},{5,4},{6,7},{7,6},{8,9},{9,8},{10,11... | collective-permute-start | bytes 786440 | tf_op jit(solution)/shard_map/ppermute | solution.py:120
  52.9 14.0 %collective-permute-start.21 = (bf16[256,512]{1,0:T(8,128)(2,1)}, bf16[256,512]{1,0:T(8,128)(2,1)S(1)}, u32[]{:S(2)}, u32[]{:S(2)}) collective-permute-start(bf16[256,512]{1,0:T(8,128)(2,1)} %get-tuple-element.58), channel_id=1, source_target_pairs={{0,96},{32,0},{64,32},{96,64},{1,97},{33,1},{65,33},{97,65},{2,98}... | collective-permute-start | bytes 786440 | tf_op jit(solution)/shard_map/ppermute | solution.py:120
  57.7 12.9 %collective-permute-start.7 = (bf16[256,512]{1,0:T(8,128)(2,1)}, bf16[256,512]{1,0:T(8,128)(2,1)S(1)}, u32[]{:S(2)}, u32[]{:S(2)}) collective-permute-start(bf16[256,512]{1,0:T(8,128)(2,1)} %get-tuple-element.40), channel_id=1, source_target_pairs={{0,32},{32,64},{64,96},{96,0},{1,33},{33,65},{65,97},{97,1},{2,34}... | collective-permute-start | bytes 786440 | tf_op jit(solution)/shard_map/ppermute | solution.py:120
  61.0 15.9 %collective-permute-start.9 = (bf16[256,512]{1,0:T(8,128)(2,1)}, bf16[256,512]{1,0:T(8,128)(2,1)S(1)}, u32[]{:S(2)}, u32[]{:S(2)}) collective-permute-start(bf16[256,512]{1,0:T(8,128)(2,1)} %get-tuple-element.42), channel_id=1, source_target_pairs={{0,96},{32,0},{64,32},{96,64},{1,97},{33,1},{65,33},{97,65},{2,98}... | collective-permute-start | bytes 786440 | tf_op jit(solution)/shard_map/ppermute | solution.py:120
  67.6 33.5 %collective-permute-start.22 = (bf16[256,512]{1,0:T(8,128)(2,1)S(1)}, bf16[256,512]{1,0:T(8,128)(2,1)S(1)}, u32[]{:S(2)}, u32[]{:S(2)}) collective-permute-start(bf16[256,512]{1,0:T(8,128)(2,1)S(1)} %get-tuple-element.60), channel_id=1, source_target_pairs={{0,8},{8,16},{16,24},{24,0},{1,9},{9,17},{17,25},{25,1},{2,10},{10... | collective-permute-start | bytes 786440 | tf_op jit(solution)/shard_map/ppermute | solution.py:120
  68.2 33.9 %collective-permute-start.23 = (bf16[256,512]{1,0:T(8,128)(2,1)S(1)}, bf16[256,512]{1,0:T(8,128)(2,1)S(1)}, u32[]{:S(2)}, u32[]{:S(2)}) collective-permute-start(bf16[256,512]{1,0:T(8,128)(2,1)S(1)} %get-tuple-element.61), channel_id=1, source_target_pairs={{0,16},{8,24},{16,0},{24,8},{1,17},{9,25},{17,1},{25,9},{2,18},{10... | collective-permute-start | bytes 786440 | tf_op jit(solution)/shard_map/ppermute | solution.py:120
  70.6 31.4 %collective-permute-start.24 = (bf16[256,512]{1,0:T(8,128)(2,1)S(1)}, bf16[256,512]{1,0:T(8,128)(2,1)S(1)}, u32[]{:S(2)}, u32[]{:S(2)}) collective-permute-start(bf16[256,512]{1,0:T(8,128)(2,1)S(1)} %get-tuple-element.62), channel_id=1, source_target_pairs={{0,24},{8,0},{16,8},{24,16},{1,25},{9,1},{17,9},{25,17},{2,26},{10... | collective-permute-start | bytes 786440 | tf_op jit(solution)/shard_map/ppermute | solution.py:120
  79.3 27.3 %collective-permute-start.10 = (bf16[256,512]{1,0:T(8,128)(2,1)}, bf16[256,512]{1,0:T(8,128)(2,1)S(1)}, u32[]{:S(2)}, u32[]{:S(2)}) collective-permute-start(bf16[256,512]{1,0:T(8,128)(2,1)} %get-tuple-element.44), channel_id=1, source_target_pairs={{0,8},{8,16},{16,24},{24,0},{1,9},{9,17},{17,25},{25,1},{2,10},{10... | collective-permute-start | bytes 786440 | tf_op jit(solution)/shard_map/ppermute | solution.py:120
  79.8 27.6 %collective-permute-start.11 = (bf16[256,512]{1,0:T(8,128)(2,1)S(1)}, bf16[256,512]{1,0:T(8,128)(2,1)S(1)}, u32[]{:S(2)}, u32[]{:S(2)}) collective-permute-start(bf16[256,512]{1,0:T(8,128)(2,1)S(1)} %get-tuple-element.45), channel_id=1, source_target_pairs={{0,16},{8,24},{16,0},{24,8},{1,17},{9,25},{17,1},{25,9},{2,18},{10... | collective-permute-start | bytes 786440 | tf_op jit(solution)/shard_map/ppermute | solution.py:120
  101.2 16.0 %collective-permute-start.12 = (bf16[256,512]{1,0:T(8,128)(2,1)S(1)}, bf16[256,512]{1,0:T(8,128)(2,1)S(1)}, u32[]{:S(2)}, u32[]{:S(2)}) collective-permute-start(bf16[256,512]{1,0:T(8,128)(2,1)S(1)} %get-tuple-element.46), channel_id=1, source_target_pairs={{0,24},{8,0},{16,8},{24,16},{1,25},{9,1},{17,9},{25,17},{2,26},{10... | collective-permute-start | bytes 786440 | tf_op jit(solution)/shard_map/ppermute | solution.py:120
  103.8 15.4 %collective-permute-start.25 = (bf16[256,512]{1,0:T(8,128)(2,1)S(1)}, bf16[256,512]{1,0:T(8,128)(2,1)S(1)}, u32[]{:S(2)}, u32[]{:S(2)}) collective-permute-start(bf16[256,512]{1,0:T(8,128)(2,1)S(1)} %get-tuple-element.64), channel_id=1, source_target_pairs={{0,8},{8,16},{16,24},{24,0},{1,9},{9,17},{17,25},{25,1},{2,10},{10... | collective-permute-start | bytes 786440 | tf_op jit(solution)/shard_map/ppermute | solution.py:120
  106.3 14.8 %collective-permute-start.26 = (bf16[256,512]{1,0:T(8,128)(2,1)S(1)}, bf16[256,512]{1,0:T(8,128)(2,1)S(1)}, u32[]{:S(2)}, u32[]{:S(2)}) collective-permute-start(bf16[256,512]{1,0:T(8,128)(2,1)S(1)} %get-tuple-element.65), channel_id=1, source_target_pairs={{0,16},{8,24},{16,0},{24,8},{1,17},{9,25},{17,1},{25,9},{2,18},{10... | collective-permute-start | bytes 786440 | tf_op jit(solution)/shard_map/ppermute | solution.py:120
  106.6 20.4 %collective-permute-start.27 = (bf16[256,512]{1,0:T(8,128)(2,1)S(1)}, bf16[256,512]{1,0:T(8,128)(2,1)S(1)}, u32[]{:S(2)}, u32[]{:S(2)}) collective-permute-start(bf16[256,512]{1,0:T(8,128)(2,1)S(1)} %get-tuple-element.66), channel_id=1, source_target_pairs={{0,24},{8,0},{16,8},{24,16},{1,25},{9,1},{17,9},{25,17},{2,26},{10... | collective-permute-start | bytes 786440 | tf_op jit(solution)/shard_map/ppermute | solution.py:120
  119.0 12.7 %collective-permute-start.13 = (bf16[256,512]{1,0:T(8,128)(2,1)S(1)}, bf16[256,512]{1,0:T(8,128)(2,1)S(1)}, u32[]{:S(2)}, u32[]{:S(2)}) collective-permute-start(bf16[256,512]{1,0:T(8,128)(2,1)S(1)} %get-tuple-element.48), channel_id=1, source_target_pairs={{0,8},{8,16},{16,24},{24,0},{1,9},{9,17},{17,25},{25,1},{2,10},{10... | collective-permute-start | bytes 786440 | tf_op jit(solution)/shard_map/ppermute | solution.py:120
  119.1 12.6 %collective-permute-start.14 = (bf16[256,512]{1,0:T(8,128)(2,1)S(1)}, bf16[256,512]{1,0:T(8,128)(2,1)S(1)}, u32[]{:S(2)}, u32[]{:S(2)}) collective-permute-start(bf16[256,512]{1,0:T(8,128)(2,1)S(1)} %get-tuple-element.49), channel_id=1, source_target_pairs={{0,16},{8,24},{16,0},{24,8},{1,17},{9,25},{17,1},{25,9},{2,18},{10... | collective-permute-start | bytes 786440 | tf_op jit(solution)/shard_map/ppermute | solution.py:120
  119.2 14.2 %collective-permute-start.15 = (bf16[256,512]{1,0:T(8,128)(2,1)S(1)}, bf16[256,512]{1,0:T(8,128)(2,1)S(1)}, u32[]{:S(2)}, u32[]{:S(2)}) collective-permute-start(bf16[256,512]{1,0:T(8,128)(2,1)S(1)} %get-tuple-element.50), channel_id=1, source_target_pairs={{0,24},{8,0},{16,8},{24,16},{1,25},{9,1},{17,9},{25,17},{2,26},{10... | collective-permute-start | bytes 786440 | tf_op jit(solution)/shard_map/ppermute | solution.py:120
  131.7 12.7 %collective-permute-start.30 = (bf16[256,512]{1,0:T(8,128)(2,1)S(1)}, bf16[256,512]{1,0:T(8,128)(2,1)S(1)}, u32[]{:S(2)}, u32[]{:S(2)}) collective-permute-start(bf16[256,512]{1,0:T(8,128)(2,1)S(1)} %get-tuple-element.70), channel_id=1, source_target_pairs={{0,96},{32,0},{64,32},{96,64},{1,97},{33,1},{65,33},{97,65},{2,98}... | collective-permute-start | bytes 786440 | tf_op jit(solution)/shard_map/ppermute | solution.py:120
  138.1 13.3 %collective-permute-start.18 = (bf16[256,512]{1,0:T(8,128)(2,1)S(1)}, bf16[256,512]{1,0:T(8,128)(2,1)S(1)}, u32[]{:S(2)}, u32[]{:S(2)}) collective-permute-start(bf16[256,512]{1,0:T(8,128)(2,1)S(1)} %get-tuple-element.54), channel_id=1, source_target_pairs={{0,96},{32,0},{64,32},{96,64},{1,97},{33,1},{65,33},{97,65},{2,98}... | collective-permute-start | bytes 786440 | tf_op jit(solution)/shard_map/ppermute | solution.py:120
  (20 other events, 154.2 us)
Sparse Core Ops, SparseCore 0:
  44.7 53.7 all-gather.1

commit v4 on v3

--- a/solution.py
+++ b/solution.py
@@ -68,28 +68,66 @@
     )(order, *operands)
 
 
+def last_kernel(skip, order, weights, *refs):
+    children, outs = refs[:-2], refs[-2:]
+    width = children[0].shape[1]
+    for s in range(2):
+        for c in range(CHUNKS):
+            total = sum(
+                jnp.dot(
+                    weights[order[2 + skip + s], order[6 + p]],
+                    children[4 * c + p][...],
+                    preferred_element_type=jnp.float32,
+                )
+                for p in DIGITS
+            )
+            outs[s][:, c * width : (c + 1) * width] = total.astype(outs[s].dtype)
+
+
+def last_level(order, weights, states, skip):
+    whole = lambda a: pl.BlockSpec(a.shape, lambda i, o: (0,) * a.ndim)
+    operands = [weights] + [block for blocks in states for block in blocks]
+    width = CHUNKS * states[0][0].shape[1]
+    return pl.pallas_call(
+        functools.partial(last_kernel, skip),
+        grid_spec=pltpu.PrefetchScalarGridSpec(
+            num_scalar_prefetch=1,
+            grid=(1,),
+            in_specs=[whole(a) for a in operands],
+            out_specs=[pl.BlockSpec((256, width), lambda i, o: (0, 0))] * 2,
+        ),
+        out_shape=[jax.ShapeDtypeStruct((256, width), jnp.bfloat16)] * 2,
+        cost_estimate=pl.CostEstimate(
+            flops=2 * 8 * 256 * 256 * width,
+            bytes_accessed=2 * (8 * 256 * 256 + 6 * 256 * width),
+            transcendentals=0,
+        ),
+        compiler_params=pltpu.CompilerParams(vmem_limit_bytes=VMEM),
+    )(order, *operands)
+
+
 def place_kernel(order, *refs):
-    blocks, out = refs[:4], refs[-1]
-    for s in DIGITS:
+    blocks, out = refs[:2], refs[-1]
+    for s in range(2):
         @pl.when(pl.program_id(0) == s)
         def _():
             out[0] = blocks[s][...]
 
 
-def place(order, blocks, chunk, into):
+def place(order, blocks, into):
     rows, width = blocks[0].shape
     extra = [] if into is None else [into]
     return pl.pallas_call(
         place_kernel,
         grid_spec=pltpu.PrefetchScalarGridSpec(
             num_scalar_prefetch=1,
-            grid=(4,),
-            in_specs=[pl.BlockSpec((rows, width), lambda i, o: (0, 0))] * 4
+            grid=(2,),
+            in_specs=[pl.BlockSpec((rows, width), lambda i, o: (0, 0))] * 2
             + [pl.BlockSpec(memory_space=pl.ANY)] * len(extra),
-            out_specs=pl.BlockSpec((1, rows, width), lambda i, o: (o[i], 0, chunk)),
-        ),
-        out_shape=jax.ShapeDtypeStruct((4, rows, CHUNKS * width), jnp.bfloat16),
-        input_output_aliases={5: 0} if extra else {},
+            out_specs=pl.BlockSpec((1, rows, width), lambda i, o: (o[i], 0, 0)),
+        ),
+        out_shape=jax.ShapeDtypeStruct((4, rows, width), jnp.bfloat16),
+        input_output_aliases={3: 0} if extra else {},
         compiler_params=pltpu.CompilerParams(vmem_limit_bytes=VMEM),
     )(order, *blocks, *extra)
 
@@ -146,11 +184,11 @@
 
 def hand_over(shards):
     first, second = lax.all_to_all(shards, "y", 1, 1, tiled=True)
-    return jnp.stack([lax.all_to_all(first, "x", 0, 0, tiled=True), second])
+    return lax.all_to_all(first, "x", 0, 0, tiled=True), second
 
 
 def all_rows(mine):
-    return lax.all_gather(mine, ("zh", "core"), axis=3, tiled=True)
+    return lax.all_gather(mine, ("zh", "core"), axis=2, tiled=True)
 
 
 def local(coefficients, transfer):
@@ -165,25 +203,28 @@
     order0 = order(b + steps, steps)
     orders = ((b - a - steps + 8) % 4).astype(jnp.int32)
     order1 = order(a + steps, a - steps + 4)
-    order2 = order(b + steps, a - steps + 4)
-    orderp = ((b - steps + 4) % 4).astype(jnp.int32)
+    odd, even = jnp.array([1, 3], jnp.int32), jnp.array([0, 2], jnp.int32)
+    order2 = order(b + jnp.concatenate([odd, even]), a - steps + 4)
 
     pieces = z_pieces(transfer[0])
     first = swap(pieces[0])
-    mine = hand_over(transfer[1:])
-    w0 = [pieces[0], first] + both_cores(pieces[1:])
-    w1, w2 = all_rows(after(mine, *w0))
+    mine1, mine2 = hand_over(transfer[1:])
+    *far, mine1 = lax.optimization_barrier((*pieces[1:], mine1))
+    w0 = [pieces[0], first] + both_cores(far)
+    w1 = all_rows(mine1)
+    w2 = all_rows(after(mine2, *w0))
     states = []
     for c in range(CHUNKS):
         blocks = exchange(level(order0, w0, [coefficients], PIECES, c, ALL_VMEM), "y")
         states.append(blocks)
     states = [exchange(select(orders, blocks), "x") for blocks in states]
     states = [exchange(level(order1, [w1], blocks), "x") for blocks in states]
-    states = [exchange(level(order2, [w2], blocks), "y") for blocks in states]
-    result = None
-    for c in range(CHUNKS):
-        result = place(orderp, states[c], c, result)
-    return result
+    one, three = last_level(order2, w2, states, 0)
+    one, three = shift(one, "y", 1), shift(three, "y", 3)
+    own, two = last_level(order2, w2, states, 2)
+    two = shift(two, "y", 2)
+    result = place((b - odd + 4) % 4, [one, three], None)
+    return place((b - even + 4) % 4, [own, two], result)
 
 
 def solution(mesh):

time: 162 us -> 162 us (level)
  starting transfers between devices: 45.5 us -> 48.9 us
  Pallas kernels: 22.9 us -> 21.1 us
    all_gather x1 -> x2, waiting for transfers between devices: 16.3 us -> 0.01 us  [all_rows(): return lax.all_gather(mine, ('zh', 'core'), axis=2, tiled=True)]
    ppermute x31 -> x28, waiting for transfers between devices: 53.2 us -> 68.5 us  [shift(): lax.ppermute(array, axis, [(i, (i + by) % size) for i in range(size)])]
    unnamed x21 -> x33, local copies, waits for them, and re-layouts: 1.83 us -> 5.78 us
    pallas_call x6 -> x4, Pallas kernels: 16.5 us -> 12.9 us  [level(): pl.pallas_call(functools.partial(level_kernel, pieces), grid_spec=pltpu.P...]
    pallas_call x0 -> x2, Pallas kernels: none -> 3.56 us  [last_level(): pl.pallas_call(functools.partial(last_kernel, skip), grid_spec=pltpu.Pref...]
    ppermute x31 -> x28, starting transfers between devices: 36.1 us -> 39.5 us  [shift(): lax.ppermute(array, axis, [(i, (i + by) % size) for i in range(size)])]
    another operation x1 -> x0, local copies, waits for them, and re-layouts: 2.65 us -> none  [local(): w1, w2 = all_rows(after(mine, *w0))]
  transfers between devices with their start and end apart: 34 -> 32, of which waited for: 15 -> 17; matrix products, arithmetic and copies ran while one was open for 4% -> 2% of each run, Pallas kernels for 13% -> 11%
where the time goes in v4:
time: 162 us
  waiting for transfers between devices  68.5 us (42%)
  starting transfers between devices  48.9 us (30%)
  Pallas kernels  21.1 us (13%)
  between operations  13.6 us (8%)
  local copies, waits for them, and re-layouts  8.67 us (5%)
    ppermute x28, waiting for transfers between devices, shift(): lax.ppermute(array, axis, [(i, (i + by) % size) for i in range(size)])  68.5 us
    ppermute x28, starting transfers between devices, shift(): lax.ppermute(array, axis, [(i, (i + by) % size) for i in range(size)])  39.5 us
    pallas_call x4, Pallas kernels, level(): pl.pallas_call(functools.partial(level_kernel, pieces), grid_spec=pltpu.P...  12.9 us
    unnamed x33, local copies, waits for them, and re-layouts  5.78 us
    all_to_all x1, starting transfers between devices, hand_over(): return (lax.all_to_all(first, 'x', 0, 0, tiled=True), second)  4.77 us
    all_to_all x1, starting transfers between devices, hand_over(): first, second = lax.all_to_all(shards, 'y', 1, 1, tiled=True)  4.68 us
    pallas_call x2, Pallas kernels, last_level(): pl.pallas_call(functools.partial(last_kernel, skip), grid_spec=pltpu.Pref...  3.56 us
  transfers between devices with their start and end apart: 32, of which 17 were waited for; matrix products, arithmetic and copies ran while one was open for 2% of the time, Pallas kernels for 11%

profile of v4, /device:TPU:62, one launch (start us, length us, event | category | flops | bytes accessed | tf_op | source)
XLA Modules:
  0.0 161.6 jit_solution(13225161394548431459)
XLA Ops:
  8.5 4.7 %all-to-all-start = ((bf16[2,4,4,32,256]{4,3,2,0,1:T(8,128)(2,1)}), bf16[2,4,4,32,256]{4,3,2,0,1:T(8,128)(2,1)S(1)}, u32[]{:S(2)}, u32[]{:S(2)}) async-start(bf16[2,4,4,32,256]{4,3,2,0,1:T(8,128)(2,1)} %copy.9), calls=%async_computation | async-start | bytes 1048576 | tf_op jit(solution)/shard_map/all_to_all | solution.py:186
  14.1 3.3 %collective-permute-start.1 = (bf16[4,4,32,256]{3,2,1,0:T(8,128)(2,1)S(1)}, bf16[4,4,32,256]{3,2,1,0:T(8,128)(2,1)S(1)}, u32[]{:S(2)}, u32[]{:S(2)}) collective-permute-start(bf16[4,4,32,256]{3,2,1,0:T(8,128)(2,1)S(1)} %slice_bitcast_fusion.2.refs_0_), channel_id=1, source_target_pairs={{0,2},{2,4},{4,6},{6,0},{1,3},{3,5},{5,7},{7,1},{8,10},{10,12},{12... | collective-permute-start | bytes 786440 | tf_op jit(solution)/shard_map/ppermute | solution.py:158
  17.5 2.2 %collective-permute-start.2 = (bf16[4,4,32,256]{3,2,1,0:T(8,128)(2,1)S(1)}, bf16[4,4,32,256]{3,2,1,0:T(8,128)(2,1)S(1)}, u32[]{:S(2)}, u32[]{:S(2)}) collective-permute-start(bf16[4,4,32,256]{3,2,1,0:T(8,128)(2,1)S(1)} %slice_bitcast_fusion.2.refs_0_), channel_id=1, source_target_pairs={{0,6},{2,0},{4,2},{6,4},{1,7},{3,1},{5,3},{7,5},{8,14},{10,8},{12,... | collective-permute-start | bytes 786440 | tf_op jit(solution)/shard_map/ppermute | solution.py:158
  19.7 4.9 %collective-permute-start.3 = (bf16[4,4,32,256]{3,2,1,0:T(8,128)(2,1)S(1)}, bf16[4,4,32,256]{3,2,1,0:T(8,128)(2,1)S(1)}, u32[]{:S(2)}, u32[]{:S(2)}) collective-permute-start(bf16[4,4,32,256]{3,2,1,0:T(8,128)(2,1)S(1)} %slice_bitcast_fusion.2.refs_0_), channel_id=1, source_target_pairs={{0,4},{2,6},{4,0},{6,2},{1,5},{3,7},{5,1},{7,3},{8,12},{10,14},{12... | collective-permute-start | bytes 786440 | tf_op jit(solution)/shard_map/ppermute | solution.py:158
  25.5 4.8 %all-to-all-start.1 = ((bf16[4,4,32,256]{3,2,1,0:T(8,128)(2,1)}), bf16[4,4,32,256]{3,2,1,0:T(8,128)(2,1)S(1)}, u32[]{:S(2)}, u32[]{:S(2)}) async-start(bf16[4,4,32,256]{3,2,1,0:T(8,128)(2,1)} %get-tuple-element.71), calls=%async_computation.1 | async-start | bytes 524288 | tf_op jit(solution)/shard_map/all_to_all | solution.py:187
  30.3 6.9 %collective-permute-done.1.refs_2_ = bf16[4,4,32,256]{3,2,1,0:T(8,128)(2,1)S(1)} collective-permute-done((bf16[4,4,32,256]{3,2,1,0:T(8,128)(2,1)S(1)}, bf16[4,4,32,256]{3,2,1,0:T(8,128)(2,1)S(1)}, u32[]{:S(2)}, u32[]{:S(2)}) %collective-permute-start.1) | collective-permute-done | bytes 262176 | tf_op jit(solution)/shard_map/ppermute | solution.py:158
  37.2 8.9 %collective-permute-done.3.refs_6_ = bf16[4,4,32,256]{3,2,1,0:T(8,128)(2,1)S(1)} collective-permute-done((bf16[4,4,32,256]{3,2,1,0:T(8,128)(2,1)S(1)}, bf16[4,4,32,256]{3,2,1,0:T(8,128)(2,1)S(1)}, u32[]{:S(2)}, u32[]{:S(2)}) %collective-permute-start.3) | collective-permute-done | bytes 262176 | tf_op jit(solution)/shard_map/ppermute | solution.py:158
  50.4 4.6 %shard_map.49 = (bf16[256,512]{1,0:T(8,128)(2,1)}, bf16[256,512]{1,0:T(8,128)(2,1)}, bf16[256,512]{1,0:T(8,128)(2,1)}, bf16[256,512]{1,0:T(8,128)(2,1)}) custom-call(s32[10]{0:T(128)} %pad_add_fusion.1.order, bf16[4,4,32,256]{3,2,1,0:T(8,128)(2,1)} %copy-done.5, bf16[4,4,32,256]{3,2,1,0:T(8,128)(2,1)} %copy-done.9, bf16[4,4,32,256]{3,2,1,0:T(8,128)(2,1)} %copy-done.6, ...), custom_call_target="tpu_custom_call" | custom-call | flops 1073741824 | bytes 4194304 | tf_op jit(solution)/shard_map/pallas_call | solution.py:52
  55.3 2.6 %collective-permute-start.17 = (bf16[256,512]{1,0:T(8,128)(2,1)}, bf16[256,512]{1,0:T(8,128)(2,1)S(1)}, u32[]{:S(2)}, u32[]{:S(2)}) collective-permute-start(bf16[256,512]{1,0:T(8,128)(2,1)} %get-tuple-element.57), channel_id=1, source_target_pairs={{0,64},{32,96},{64,0},{96,32},{1,65},{33,97},{65,1},{97,33},{2,66}... | collective-permute-start | bytes 786440 | tf_op jit(solution)/shard_map/ppermute | solution.py:158
  57.9 4.8 %shard_map.46 = (bf16[256,512]{1,0:T(8,128)(2,1)}, bf16[256,512]{1,0:T(8,128)(2,1)}, bf16[256,512]{1,0:T(8,128)(2,1)}, bf16[256,512]{1,0:T(8,128)(2,1)}) custom-call(s32[10]{0:T(128)} %pad_add_fusion.1.order, bf16[4,4,32,256]{3,2,1,0:T(8,128)(2,1)} %copy-done.5, bf16[4,4,32,256]{3,2,1,0:T(8,128)(2,1)} %copy-done.9, bf16[4,4,32,256]{3,2,1,0:T(8,128)(2,1)} %copy-done.6, ...), custom_call_target="tpu_custom_call" | custom-call | flops 1073741824 | bytes 4194304 | tf_op jit(solution)/shard_map/pallas_call | solution.py:52
  62.7 3.1 %collective-permute-start.7 = (bf16[256,512]{1,0:T(8,128)(2,1)}, bf16[256,512]{1,0:T(8,128)(2,1)S(1)}, u32[]{:S(2)}, u32[]{:S(2)}) collective-permute-start(bf16[256,512]{1,0:T(8,128)(2,1)} %get-tuple-element.44), channel_id=1, source_target_pairs={{0,32},{32,64},{64,96},{96,0},{1,33},{33,65},{65,97},{97,1},{2,34}... | collective-permute-start | bytes 786440 | tf_op jit(solution)/shard_map/ppermute | solution.py:158
  67.3 4.6 %collective-permute-done.18.refs_3_ = bf16[256,512]{1,0:T(8,128)(2,1)S(1)} collective-permute-done((bf16[256,512]{1,0:T(8,128)(2,1)}, bf16[256,512]{1,0:T(8,128)(2,1)S(1)}, u32[]{:S(2)}, u32[]{:S(2)}) %collective-permute-start.18) | collective-permute-done | bytes 262176 | tf_op jit(solution)/shard_map/ppermute | solution.py:158
  73.2 2.4 %collective-permute-start.20 = (bf16[256,512]{1,0:T(8,128)(2,1)S(1)}, bf16[256,512]{1,0:T(8,128)(2,1)S(1)}, u32[]{:S(2)}, u32[]{:S(2)}) collective-permute-start(bf16[256,512]{1,0:T(8,128)(2,1)S(1)} %get-tuple-element.61), channel_id=1, source_target_pairs={{0,16},{8,24},{16,0},{24,8},{1,17},{9,25},{17,1},{25,9},{2,18},{10... | collective-permute-start | bytes 786440 | tf_op jit(solution)/shard_map/ppermute | solution.py:158
  77.5 4.5 %collective-permute-done.9.refs_3_ = bf16[256,512]{1,0:T(8,128)(2,1)S(1)} collective-permute-done((bf16[256,512]{1,0:T(8,128)(2,1)}, bf16[256,512]{1,0:T(8,128)(2,1)S(1)}, u32[]{:S(2)}, u32[]{:S(2)}) %collective-permute-start.9) | collective-permute-done | bytes 262176 | tf_op jit(solution)/shard_map/ppermute | solution.py:158
  84.2 2.4 %collective-permute-start.11 = (bf16[256,512]{1,0:T(8,128)(2,1)S(1)}, bf16[256,512]{1,0:T(8,128)(2,1)S(1)}, u32[]{:S(2)}, u32[]{:S(2)}) collective-permute-start(bf16[256,512]{1,0:T(8,128)(2,1)S(1)} %get-tuple-element.49), channel_id=1, source_target_pairs={{0,16},{8,24},{16,0},{24,8},{1,17},{9,25},{17,1},{25,9},{2,18},{10... | collective-permute-start | bytes 786440 | tf_op jit(solution)/shard_map/ppermute | solution.py:158
  94.9 5.7 %collective-permute-done.12.refs_4_ = bf16[256,512]{1,0:T(8,128)(2,1)S(1)} collective-permute-done((bf16[256,512]{1,0:T(8,128)(2,1)S(1)}, bf16[256,512]{1,0:T(8,128)(2,1)S(1)}, u32[]{:S(2)}, u32[]{:S(2)}) %collective-permute-start.12) | collective-permute-done | bytes 262176 | tf_op jit(solution)/shard_map/ppermute | solution.py:158
  100.6 1.8 %shard_map.48 = (bf16[256,512]{1,0:T(8,128)(2,1)S(1)}, bf16[256,512]{1,0:T(8,128)(2,1)S(1)}, bf16[256,512]{1,0:T(8,128)(2,1)S(1)}, bf16[256,512]{1,0:T(8,128)(2,1)S(1)}) custom-call(s32[10]{0:T(128)S(1)} %get-tuple-element.73.order, bf16[4,4,256,256]{3,2,1,0:T(8,128)(2,1)S(1)} %copy-done.4, bf16[256,512]{1,0:T(8,128)(2,1)S(1)} %get-tuple-element.47.refs_1_, ...), custom_call_target="tpu_custom_call" | custom-call | flops 1073741824 | bytes 4194304 | tf_op jit(solution)/shard_map/pallas_call | solution.py:52
  103.1 5.5 %collective-permute-start.14 = (bf16[256,512]{1,0:T(8,128)(2,1)S(1)}, bf16[256,512]{1,0:T(8,128)(2,1)S(1)}, u32[]{:S(2)}, u32[]{:S(2)}) collective-permute-start(bf16[256,512]{1,0:T(8,128)(2,1)S(1)} %get-tuple-element.53), channel_id=1, source_target_pairs={{0,16},{8,24},{16,0},{24,8},{1,17},{9,25},{17,1},{25,9},{2,18},{10... | collective-permute-start | bytes 786440 | tf_op jit(solution)/shard_map/ppermute | solution.py:158
  109.9 2.0 %collective-permute-done.24.refs_7_ = bf16[256,512]{1,0:T(8,128)(2,1)S(1)} collective-permute-done((bf16[256,512]{1,0:T(8,128)(2,1)S(1)}, bf16[256,512]{1,0:T(8,128)(2,1)S(1)}, u32[]{:S(2)}, u32[]{:S(2)}) %collective-permute-start.24) | collective-permute-done | bytes 262176 | tf_op jit(solution)/shard_map/ppermute | solution.py:158
  111.9 3.6 %collective-permute-done.13.refs_1_ = bf16[256,512]{1,0:T(8,128)(2,1)S(1)} collective-permute-done((bf16[256,512]{1,0:T(8,128)(2,1)S(1)}, bf16[256,512]{1,0:T(8,128)(2,1)S(1)}, u32[]{:S(2)}, u32[]{:S(2)}) %collective-permute-start.13) | collective-permute-done | bytes 262176 | tf_op jit(solution)/shard_map/ppermute | solution.py:158
  115.4 2.1 %collective-permute-done.14.refs_2_ = bf16[256,512]{1,0:T(8,128)(2,1)S(1)} collective-permute-done((bf16[256,512]{1,0:T(8,128)(2,1)S(1)}, bf16[256,512]{1,0:T(8,128)(2,1)S(1)}, u32[]{:S(2)}, u32[]{:S(2)}) %collective-permute-start.14) | collective-permute-done | bytes 262176 | tf_op jit(solution)/shard_map/ppermute | solution.py:158
  117.5 4.4 %collective-permute-done.15.refs_3_ = bf16[256,512]{1,0:T(8,128)(2,1)S(1)} collective-permute-done((bf16[256,512]{1,0:T(8,128)(2,1)S(1)}, bf16[256,512]{1,0:T(8,128)(2,1)S(1)}, u32[]{:S(2)}, u32[]{:S(2)}) %collective-permute-start.15) | collective-permute-done | bytes 262176 | tf_op jit(solution)/shard_map/ppermute | solution.py:158
  129.9 10.3 %collective-permute-done.26.refs_0_ = bf16[256,1024]{1,0:T(8,128)(2,1)S(1)} collective-permute-done((bf16[256,1024]{1,0:T(8,128)(2,1)S(1)}, bf16[256,1024]{1,0:T(8,128)(2,1)S(1)}, u32[]{:S(2)}, u32[]{:S(2)}) %collective-permute-start.26) | collective-permute-done | bytes 524320 | tf_op jit(solution)/shard_map/ppermute | solution.py:158
  140.2 11.4 %collective-permute-done.27.refs_1_ = bf16[256,1024]{1,0:T(8,128)(2,1)S(1)} collective-permute-done((bf16[256,1024]{1,0:T(8,128)(2,1)S(1)}, bf16[256,1024]{1,0:T(8,128)(2,1)S(1)}, u32[]{:S(2)}, u32[]{:S(2)}) %collective-permute-start.27) | collective-permute-done | bytes 524320 | tf_op jit(solution)/shard_map/ppermute | solution.py:158
  (96 shorter events, 36.6 us)
Async XLA Ops:
  8.5 16.2 %all-to-all-start = ((bf16[2,4,4,32,256]{4,3,2,0,1:T(8,128)(2,1)}), bf16[2,4,4,32,256]{4,3,2,0,1:T(8,128)(2,1)S(1)}, u32[]{:S(2)}, u32[]{:S(2)}) async-start(bf16[2,4,4,32,256]{4,3,2,0,1:T(8,128)(2,1)} %copy.9), calls=%async_computation | async-start | bytes 1048576 | tf_op jit(solution)/shard_map/all_to_all | solution.py:186
  14.1 23.0 %collective-permute-start.1 = (bf16[4,4,32,256]{3,2,1,0:T(8,128)(2,1)S(1)}, bf16[4,4,32,256]{3,2,1,0:T(8,128)(2,1)S(1)}, u32[]{:S(2)}, u32[]{:S(2)}) collective-permute-start(bf16[4,4,32,256]{3,2,1,0:T(8,128)(2,1)S(1)} %slice_bitcast_fusion.2.refs_0_), channel_id=1, source_target_pairs={{0,2},{2,4},{4,6},{6,0},{1,3},{3,5},{5,7},{7,1},{8,10},{10,12},{12... | collective-permute-start | bytes 786440 | tf_op jit(solution)/shard_map/ppermute | solution.py:158
  17.5 19.7 %collective-permute-start.2 = (bf16[4,4,32,256]{3,2,1,0:T(8,128)(2,1)S(1)}, bf16[4,4,32,256]{3,2,1,0:T(8,128)(2,1)S(1)}, u32[]{:S(2)}, u32[]{:S(2)}) collective-permute-start(bf16[4,4,32,256]{3,2,1,0:T(8,128)(2,1)S(1)} %slice_bitcast_fusion.2.refs_0_), channel_id=1, source_target_pairs={{0,6},{2,0},{4,2},{6,4},{1,7},{3,1},{5,3},{7,5},{8,14},{10,8},{12,... | collective-permute-start | bytes 786440 | tf_op jit(solution)/shard_map/ppermute | solution.py:158
  19.7 26.4 %collective-permute-start.3 = (bf16[4,4,32,256]{3,2,1,0:T(8,128)(2,1)S(1)}, bf16[4,4,32,256]{3,2,1,0:T(8,128)(2,1)S(1)}, u32[]{:S(2)}, u32[]{:S(2)}) collective-permute-start(bf16[4,4,32,256]{3,2,1,0:T(8,128)(2,1)S(1)} %slice_bitcast_fusion.2.refs_0_), channel_id=1, source_target_pairs={{0,4},{2,6},{4,0},{6,2},{1,5},{3,7},{5,1},{7,3},{8,12},{10,14},{12... | collective-permute-start | bytes 786440 | tf_op jit(solution)/shard_map/ppermute | solution.py:158
  25.5 20.6 %all-to-all-start.1 = ((bf16[4,4,32,256]{3,2,1,0:T(8,128)(2,1)}), bf16[4,4,32,256]{3,2,1,0:T(8,128)(2,1)S(1)}, u32[]{:S(2)}, u32[]{:S(2)}) async-start(bf16[4,4,32,256]{3,2,1,0:T(8,128)(2,1)} %get-tuple-element.71), calls=%async_computation.1 | async-start | bytes 524288 | tf_op jit(solution)/shard_map/all_to_all | solution.py:187
  30.3 58.0 %all-gather.5.cloned.1.call-start = ((), (), s32[]{:S(2)}) async-start(), calls=%async_computation.3 | async-start | bytes 2359296 | tf_op jit(solution)/shard_map/all_gather | solution.py:191
  46.9 75.0 %all-gather.3.cloned.1.call-start = ((), (), s32[]{:S(2)}) async-start(), calls=%async_computation.2 | async-start | bytes 2359296 | tf_op jit(solution)/shard_map/all_gather | solution.py:191
  55.3 12.1 %collective-permute-start.17 = (bf16[256,512]{1,0:T(8,128)(2,1)}, bf16[256,512]{1,0:T(8,128)(2,1)S(1)}, u32[]{:S(2)}, u32[]{:S(2)}) collective-permute-start(bf16[256,512]{1,0:T(8,128)(2,1)} %get-tuple-element.57), channel_id=1, source_target_pairs={{0,64},{32,96},{64,0},{96,32},{1,65},{33,97},{65,1},{97,33},{2,66}... | collective-permute-start | bytes 786440 | tf_op jit(solution)/shard_map/ppermute | solution.py:158
  57.9 14.0 %collective-permute-start.18 = (bf16[256,512]{1,0:T(8,128)(2,1)}, bf16[256,512]{1,0:T(8,128)(2,1)S(1)}, u32[]{:S(2)}, u32[]{:S(2)}) collective-permute-start(bf16[256,512]{1,0:T(8,128)(2,1)} %get-tuple-element.58), channel_id=1, source_target_pairs={{0,96},{32,0},{64,32},{96,64},{1,97},{33,1},{65,33},{97,65},{2,98}... | collective-permute-start | bytes 786440 | tf_op jit(solution)/shard_map/ppermute | solution.py:158
  62.7 12.9 %collective-permute-start.7 = (bf16[256,512]{1,0:T(8,128)(2,1)}, bf16[256,512]{1,0:T(8,128)(2,1)S(1)}, u32[]{:S(2)}, u32[]{:S(2)}) collective-permute-start(bf16[256,512]{1,0:T(8,128)(2,1)} %get-tuple-element.44), channel_id=1, source_target_pairs={{0,32},{32,64},{64,96},{96,0},{1,33},{33,65},{65,97},{97,1},{2,34}... | collective-permute-start | bytes 786440 | tf_op jit(solution)/shard_map/ppermute | solution.py:158
  65.9 16.0 %collective-permute-start.9 = (bf16[256,512]{1,0:T(8,128)(2,1)}, bf16[256,512]{1,0:T(8,128)(2,1)S(1)}, u32[]{:S(2)}, u32[]{:S(2)}) collective-permute-start(bf16[256,512]{1,0:T(8,128)(2,1)} %get-tuple-element.46), channel_id=1, source_target_pairs={{0,96},{32,0},{64,32},{96,64},{1,97},{33,1},{65,33},{97,65},{2,98}... | collective-permute-start | bytes 786440 | tf_op jit(solution)/shard_map/ppermute | solution.py:158
  72.6 14.0 %collective-permute-start.19 = (bf16[256,512]{1,0:T(8,128)(2,1)S(1)}, bf16[256,512]{1,0:T(8,128)(2,1)S(1)}, u32[]{:S(2)}, u32[]{:S(2)}) collective-permute-start(bf16[256,512]{1,0:T(8,128)(2,1)S(1)} %get-tuple-element.60), channel_id=1, source_target_pairs={{0,8},{8,16},{16,24},{24,0},{1,9},{9,17},{17,25},{25,1},{2,10},{10... | collective-permute-start | bytes 786440 | tf_op jit(solution)/shard_map/ppermute | solution.py:158
  73.2 13.4 %collective-permute-start.20 = (bf16[256,512]{1,0:T(8,128)(2,1)S(1)}, bf16[256,512]{1,0:T(8,128)(2,1)S(1)}, u32[]{:S(2)}, u32[]{:S(2)}) collective-permute-start(bf16[256,512]{1,0:T(8,128)(2,1)S(1)} %get-tuple-element.61), channel_id=1, source_target_pairs={{0,16},{8,24},{16,0},{24,8},{1,17},{9,25},{17,1},{25,9},{2,18},{10... | collective-permute-start | bytes 786440 | tf_op jit(solution)/shard_map/ppermute | solution.py:158
  75.6 12.7 %collective-permute-start.21 = (bf16[256,512]{1,0:T(8,128)(2,1)S(1)}, bf16[256,512]{1,0:T(8,128)(2,1)S(1)}, u32[]{:S(2)}, u32[]{:S(2)}) collective-permute-start(bf16[256,512]{1,0:T(8,128)(2,1)S(1)} %get-tuple-element.62), channel_id=1, source_target_pairs={{0,24},{8,0},{16,8},{24,16},{1,25},{9,1},{17,9},{25,17},{2,26},{10... | collective-permute-start | bytes 786440 | tf_op jit(solution)/shard_map/ppermute | solution.py:158
  86.6 14.0 %collective-permute-start.12 = (bf16[256,512]{1,0:T(8,128)(2,1)S(1)}, bf16[256,512]{1,0:T(8,128)(2,1)S(1)}, u32[]{:S(2)}, u32[]{:S(2)}) collective-permute-start(bf16[256,512]{1,0:T(8,128)(2,1)S(1)} %get-tuple-element.50), channel_id=1, source_target_pairs={{0,24},{8,0},{16,8},{24,16},{1,25},{9,1},{17,9},{25,17},{2,26},{10... | collective-permute-start | bytes 786440 | tf_op jit(solution)/shard_map/ppermute | solution.py:158
  91.7 16.9 %collective-permute-start.22 = (bf16[256,512]{1,0:T(8,128)(2,1)S(1)}, bf16[256,512]{1,0:T(8,128)(2,1)S(1)}, u32[]{:S(2)}, u32[]{:S(2)}) collective-permute-start(bf16[256,512]{1,0:T(8,128)(2,1)S(1)} %get-tuple-element.64), channel_id=1, source_target_pairs={{0,8},{8,16},{16,24},{24,0},{1,9},{9,17},{17,25},{25,1},{2,10},{10... | collective-permute-start | bytes 786440 | tf_op jit(solution)/shard_map/ppermute | solution.py:158
  93.3 16.6 %collective-permute-start.23 = (bf16[256,512]{1,0:T(8,128)(2,1)S(1)}, bf16[256,512]{1,0:T(8,128)(2,1)S(1)}, u32[]{:S(2)}, u32[]{:S(2)}) collective-permute-start(bf16[256,512]{1,0:T(8,128)(2,1)S(1)} %get-tuple-element.65), channel_id=1, source_target_pairs={{0,16},{8,24},{16,0},{24,8},{1,17},{9,25},{17,1},{25,9},{2,18},{10... | collective-permute-start | bytes 786440 | tf_op jit(solution)/shard_map/ppermute | solution.py:158
  94.7 17.2 %collective-permute-start.24 = (bf16[256,512]{1,0:T(8,128)(2,1)S(1)}, bf16[256,512]{1,0:T(8,128)(2,1)S(1)}, u32[]{:S(2)}, u32[]{:S(2)}) collective-permute-start(bf16[256,512]{1,0:T(8,128)(2,1)S(1)} %get-tuple-element.66), channel_id=1, source_target_pairs={{0,24},{8,0},{16,8},{24,16},{1,25},{9,1},{17,9},{25,17},{2,26},{10... | collective-permute-start | bytes 786440 | tf_op jit(solution)/shard_map/ppermute | solution.py:158
  102.4 13.0 %collective-permute-start.13 = (bf16[256,512]{1,0:T(8,128)(2,1)S(1)}, bf16[256,512]{1,0:T(8,128)(2,1)S(1)}, u32[]{:S(2)}, u32[]{:S(2)}) collective-permute-start(bf16[256,512]{1,0:T(8,128)(2,1)S(1)} %get-tuple-element.52), channel_id=1, source_target_pairs={{0,8},{8,16},{16,24},{24,0},{1,9},{9,17},{17,25},{25,1},{2,10},{10... | collective-permute-start | bytes 786440 | tf_op jit(solution)/shard_map/ppermute | solution.py:158
  103.1 14.4 %collective-permute-start.14 = (bf16[256,512]{1,0:T(8,128)(2,1)S(1)}, bf16[256,512]{1,0:T(8,128)(2,1)S(1)}, u32[]{:S(2)}, u32[]{:S(2)}) collective-permute-start(bf16[256,512]{1,0:T(8,128)(2,1)S(1)} %get-tuple-element.53), channel_id=1, source_target_pairs={{0,16},{8,24},{16,0},{24,8},{1,17},{9,25},{17,1},{25,9},{2,18},{10... | collective-permute-start | bytes 786440 | tf_op jit(solution)/shard_map/ppermute | solution.py:158
  108.6 13.4 %collective-permute-start.15 = (bf16[256,512]{1,0:T(8,128)(2,1)S(1)}, bf16[256,512]{1,0:T(8,128)(2,1)S(1)}, u32[]{:S(2)}, u32[]{:S(2)}) collective-permute-start(bf16[256,512]{1,0:T(8,128)(2,1)S(1)} %get-tuple-element.54), channel_id=1, source_target_pairs={{0,24},{8,0},{16,8},{24,16},{1,25},{9,1},{17,9},{25,17},{2,26},{10... | collective-permute-start | bytes 786440 | tf_op jit(solution)/shard_map/ppermute | solution.py:158
  125.3 14.9 %collective-permute-start.26 = (bf16[256,1024]{1,0:T(8,128)(2,1)S(1)}, bf16[256,1024]{1,0:T(8,128)(2,1)S(1)}, u32[]{:S(2)}, u32[]{:S(2)}) collective-permute-start(bf16[256,1024]{1,0:T(8,128)(2,1)S(1)} %get-tuple-element.69), channel_id=1, source_target_pairs={{0,32},{32,64},{64,96},{96,0},{1,33},{33,65},{65,97},{97,1},{2,34}... | collective-permute-start | bytes 1572872 | tf_op jit(solution)/shard_map/ppermute | solution.py:158
  125.7 26.0 %collective-permute-start.27 = (bf16[256,1024]{1,0:T(8,128)(2,1)S(1)}, bf16[256,1024]{1,0:T(8,128)(2,1)S(1)}, u32[]{:S(2)}, u32[]{:S(2)}) collective-permute-start(bf16[256,1024]{1,0:T(8,128)(2,1)S(1)} %get-tuple-element.70), channel_id=1, source_target_pairs={{0,96},{32,0},{64,32},{96,64},{1,97},{33,1},{65,33},{97,65},{2,98}... | collective-permute-start | bytes 1572872 | tf_op jit(solution)/shard_map/ppermute | solution.py:158
  129.2 24.0 %collective-permute-start.25 = (bf16[256,1024]{1,0:T(8,128)(2,1)S(1)}, bf16[256,1024]{1,0:T(8,128)(2,1)S(1)}, u32[]{:S(2)}, u32[]{:S(2)}) collective-permute-start(bf16[256,1024]{1,0:T(8,128)(2,1)S(1)} %get-tuple-element.68), channel_id=1, source_target_pairs={{0,64},{32,96},{64,0},{96,32},{1,65},{33,97},{65,1},{97,33},{2,66}... | collective-permute-start | bytes 1572872 | tf_op jit(solution)/shard_map/ppermute | solution.py:158
  (24 other events, 175.9 us)
Sparse Core Ops, SparseCore 0:
  47.0 33.2 all-gather.4
  82.2 33.9 all-gather.2

commit v5 on v4

--- a/solution.py
+++ b/solution.py
@@ -215,7 +215,7 @@
     w2 = all_rows(after(mine2, *w0))
     states = []
     for c in range(CHUNKS):
-        blocks = exchange(level(order0, w0, [coefficients], PIECES, c, ALL_VMEM), "y")
+        blocks = exchange(level(order0, w0, [coefficients], PIECES, c, VMEM if c else ALL_VMEM), "y")
         states.append(blocks)
     states = [exchange(select(orders, blocks), "x") for blocks in states]
     states = [exchange(level(order1, [w1], blocks), "x") for blocks in states]

time: 162 us -> 165 us (1.019)
  local copies, waits for them, and re-layouts: 8.67 us -> 15.4 us
  waiting for transfers between devices: 68.5 us -> 66.5 us
  Pallas kernels: 21.1 us -> 19.2 us
    unnamed x33 -> x45, local copies, waits for them, and re-layouts: 5.78 us -> 11.5 us
    ppermute x28, waiting for transfers between devices: 68.5 us -> 66.5 us  [shift(): lax.ppermute(array, axis, [(i, (i + by) % size) for i in range(size)])]
    pallas_call x4, Pallas kernels: 12.9 us -> 11 us  [level(): pl.pallas_call(functools.partial(level_kernel, pieces), grid_spec=pltpu.P...]
  transfers between devices with their start and end apart: 32 -> 32, of which waited for: 17 -> 15; matrix products, arithmetic and copies ran while one was open for 2% -> 2% of each run, Pallas kernels for 11% -> 10%
where the time goes in v5:
time: 165 us; the launch traced here: 164 us
  waiting for transfers between devices  66.5 us (40%)
  starting transfers between devices  49.4 us (30%)
  Pallas kernels  19.2 us (12%)
  local copies, waits for them, and re-layouts  15.4 us (9%)
  between operations  13.6 us (8%)
    ppermute x28, waiting for transfers between devices, shift(): lax.ppermute(array, axis, [(i, (i + by) % size) for i in range(size)])  66.5 us
    ppermute x28, starting transfers between devices, shift(): lax.ppermute(array, axis, [(i, (i + by) % size) for i in range(size)])  39.8 us
    unnamed x45, local copies, waits for them, and re-layouts  11.5 us
    pallas_call x4, Pallas kernels, level(): pl.pallas_call(functools.partial(level_kernel, pieces), grid_spec=pltpu.P...  11 us
    all_to_all x1, starting transfers between devices, hand_over(): first, second = lax.all_to_all(shards, 'y', 1, 1, tiled=True)  4.82 us
    all_to_all x1, starting transfers between devices, hand_over(): return (lax.all_to_all(first, 'x', 0, 0, tiled=True), second)  4.77 us
    pallas_call x2, Pallas kernels, last_level(): pl.pallas_call(functools.partial(last_kernel, skip), grid_spec=pltpu.Pref...  3.56 us
  transfers between devices with their start and end apart: 32, of which 15 were waited for; matrix products, arithmetic and copies ran while one was open for 2% of the time, Pallas kernels for 10%

profile of v5, /device:TPU:62, one launch (start us, length us, event | category | flops | bytes accessed | tf_op | source)
XLA Modules:
  0.0 164.4 jit_solution(11562926043647061888)
XLA Ops:
  8.5 4.8 %all-to-all-start = ((bf16[2,4,4,32,256]{4,3,2,0,1:T(8,128)(2,1)}), bf16[2,4,4,32,256]{4,3,2,0,1:T(8,128)(2,1)}, u32[]{:S(2)}, u32[]{:S(2)}) async-start(bf16[2,4,4,32,256]{4,3,2,0,1:T(8,128)(2,1)} %copy.9), calls=%async_computation | async-start | bytes 1048576 | tf_op jit(solution)/shard_map/all_to_all | solution.py:186
  14.3 3.3 %collective-permute-start.1 = (bf16[4,4,32,256]{3,2,1,0:T(8,128)(2,1)S(1)}, bf16[4,4,32,256]{3,2,1,0:T(8,128)(2,1)S(1)}, u32[]{:S(2)}, u32[]{:S(2)}) collective-permute-start(bf16[4,4,32,256]{3,2,1,0:T(8,128)(2,1)S(1)} %slice_bitcast_fusion.2.refs_0_), channel_id=1, source_target_pairs={{0,2},{2,4},{4,6},{6,0},{1,3},{3,5},{5,7},{7,1},{8,10},{10,12},{12... | collective-permute-start | bytes 786440 | tf_op jit(solution)/shard_map/ppermute | solution.py:158
  17.6 2.2 %collective-permute-start.2 = (bf16[4,4,32,256]{3,2,1,0:T(8,128)(2,1)S(1)}, bf16[4,4,32,256]{3,2,1,0:T(8,128)(2,1)S(1)}, u32[]{:S(2)}, u32[]{:S(2)}) collective-permute-start(bf16[4,4,32,256]{3,2,1,0:T(8,128)(2,1)S(1)} %slice_bitcast_fusion.2.refs_0_), channel_id=1, source_target_pairs={{0,6},{2,0},{4,2},{6,4},{1,7},{3,1},{5,3},{7,5},{8,14},{10,8},{12,... | collective-permute-start | bytes 786440 | tf_op jit(solution)/shard_map/ppermute | solution.py:158
  19.8 4.9 %collective-permute-start.3 = (bf16[4,4,32,256]{3,2,1,0:T(8,128)(2,1)S(1)}, bf16[4,4,32,256]{3,2,1,0:T(8,128)(2,1)S(1)}, u32[]{:S(2)}, u32[]{:S(2)}) collective-permute-start(bf16[4,4,32,256]{3,2,1,0:T(8,128)(2,1)S(1)} %slice_bitcast_fusion.2.refs_0_), channel_id=1, source_target_pairs={{0,4},{2,6},{4,0},{6,2},{1,5},{3,7},{5,1},{7,3},{8,12},{10,14},{12... | collective-permute-start | bytes 786440 | tf_op jit(solution)/shard_map/ppermute | solution.py:158
  24.8 1.9 %slice_bitcast_fusion = (bf16[4,4,32,256]{3,2,1,0:T(8,128)(2,1)}, bf16[4,4,32,256]{3,2,1,0:T(8,128)(2,1)}) fusion(bf16[2,4,4,32,256]{4,3,2,0,1:T(8,128)(2,1)} %all-to-all-done), kind=kLoop, calls=%fused_computation | loop fusion | bytes 1048576 | tf_op jit(solution)/shard_map/unstack | solution.py:186
  26.7 4.8 %all-to-all-start.1 = ((bf16[4,4,32,256]{3,2,1,0:T(8,128)(2,1)}), bf16[4,4,32,256]{3,2,1,0:T(8,128)(2,1)S(1)}, u32[]{:S(2)}, u32[]{:S(2)}) async-start(bf16[4,4,32,256]{3,2,1,0:T(8,128)(2,1)} %get-tuple-element.71), calls=%async_computation.1 | async-start | bytes 524288 | tf_op jit(solution)/shard_map/all_to_all | solution.py:187
  31.4 6.0 %collective-permute-done.1.refs_2_ = bf16[4,4,32,256]{3,2,1,0:T(8,128)(2,1)S(1)} collective-permute-done((bf16[4,4,32,256]{3,2,1,0:T(8,128)(2,1)S(1)}, bf16[4,4,32,256]{3,2,1,0:T(8,128)(2,1)S(1)}, u32[]{:S(2)}, u32[]{:S(2)}) %collective-permute-start.1) | collective-permute-done | bytes 262176 | tf_op jit(solution)/shard_map/ppermute | solution.py:158
  37.4 8.8 %collective-permute-done.3.refs_6_ = bf16[4,4,32,256]{3,2,1,0:T(8,128)(2,1)S(1)} collective-permute-done((bf16[4,4,32,256]{3,2,1,0:T(8,128)(2,1)S(1)}, bf16[4,4,32,256]{3,2,1,0:T(8,128)(2,1)S(1)}, u32[]{:S(2)}, u32[]{:S(2)}) %collective-permute-start.3) | collective-permute-done | bytes 262176 | tf_op jit(solution)/shard_map/ppermute | solution.py:158
  54.2 2.7 %shard_map.49 = (bf16[256,512]{1,0:T(8,128)(2,1)S(1)}, bf16[256,512]{1,0:T(8,128)(2,1)}, bf16[256,512]{1,0:T(8,128)(2,1)}, bf16[256,512]{1,0:T(8,128)(2,1)}) custom-call(s32[10]{0:T(128)S(1)} %pad_add_fusion.1.order, bf16[4,4,32,256]{3,2,1,0:T(8,128)(2,1)S(1)} %slice_bitcast_fusion.2.refs_0_, bf16[4,4,32,256]{3,2,1,0:T(8,128)(2,1)S(1)} %collective-permute-done.refs_1_, ...), custom_call_target="tpu_custom_call" | custom-call | flops 1073741824 | bytes 4194304 | tf_op jit(solution)/shard_map/pallas_call | solution.py:52
  57.9 2.6 %collective-permute-start.17 = (bf16[256,512]{1,0:T(8,128)(2,1)}, bf16[256,512]{1,0:T(8,128)(2,1)S(1)}, u32[]{:S(2)}, u32[]{:S(2)}) collective-permute-start(bf16[256,512]{1,0:T(8,128)(2,1)} %get-tuple-element.57), channel_id=1, source_target_pairs={{0,64},{32,96},{64,0},{96,32},{1,65},{33,97},{65,1},{97,33},{2,66}... | collective-permute-start | bytes 786440 | tf_op jit(solution)/shard_map/ppermute | solution.py:158
  60.6 4.8 %shard_map.46 = (bf16[256,512]{1,0:T(8,128)(2,1)}, bf16[256,512]{1,0:T(8,128)(2,1)}, bf16[256,512]{1,0:T(8,128)(2,1)}, bf16[256,512]{1,0:T(8,128)(2,1)}) custom-call(s32[10]{0:T(128)} %copy-done.16, bf16[4,4,32,256]{3,2,1,0:T(8,128)(2,1)} %copy-done.2, bf16[4,4,32,256]{3,2,1,0:T(8,128)(2,1)} %copy-done.6, bf16[4,4,32,256]{3,2,1,0:T(8,128)(2,1)} %copy-done.3, ...), custom_call_target="tpu_custom_call" | custom-call | flops 1073741824 | bytes 4194304 | tf_op jit(solution)/shard_map/pallas_call | solution.py:52
  65.4 3.1 %collective-permute-start.7 = (bf16[256,512]{1,0:T(8,128)(2,1)}, bf16[256,512]{1,0:T(8,128)(2,1)S(1)}, u32[]{:S(2)}, u32[]{:S(2)}) collective-permute-start(bf16[256,512]{1,0:T(8,128)(2,1)} %get-tuple-element.44), channel_id=1, source_target_pairs={{0,32},{32,64},{64,96},{96,0},{1,33},{33,65},{65,97},{97,1},{2,34}... | collective-permute-start | bytes 786440 | tf_op jit(solution)/shard_map/ppermute | solution.py:158
  70.0 4.5 %collective-permute-done.18.refs_3_ = bf16[256,512]{1,0:T(8,128)(2,1)S(1)} collective-permute-done((bf16[256,512]{1,0:T(8,128)(2,1)}, bf16[256,512]{1,0:T(8,128)(2,1)S(1)}, u32[]{:S(2)}, u32[]{:S(2)}) %collective-permute-start.18) | collective-permute-done | bytes 262176 | tf_op jit(solution)/shard_map/ppermute | solution.py:158
  76.0 2.4 %collective-permute-start.20 = (bf16[256,512]{1,0:T(8,128)(2,1)S(1)}, bf16[256,512]{1,0:T(8,128)(2,1)S(1)}, u32[]{:S(2)}, u32[]{:S(2)}) collective-permute-start(bf16[256,512]{1,0:T(8,128)(2,1)S(1)} %get-tuple-element.61), channel_id=1, source_target_pairs={{0,16},{8,24},{16,0},{24,8},{1,17},{9,25},{17,1},{25,9},{2,18},{10... | collective-permute-start | bytes 786440 | tf_op jit(solution)/shard_map/ppermute | solution.py:158
  80.1 4.4 %collective-permute-done.9.refs_3_ = bf16[256,512]{1,0:T(8,128)(2,1)S(1)} collective-permute-done((bf16[256,512]{1,0:T(8,128)(2,1)}, bf16[256,512]{1,0:T(8,128)(2,1)S(1)}, u32[]{:S(2)}, u32[]{:S(2)}) %collective-permute-start.9) | collective-permute-done | bytes 262176 | tf_op jit(solution)/shard_map/ppermute | solution.py:158
  86.8 2.4 %collective-permute-start.11 = (bf16[256,512]{1,0:T(8,128)(2,1)S(1)}, bf16[256,512]{1,0:T(8,128)(2,1)S(1)}, u32[]{:S(2)}, u32[]{:S(2)}) collective-permute-start(bf16[256,512]{1,0:T(8,128)(2,1)S(1)} %get-tuple-element.49), channel_id=1, source_target_pairs={{0,16},{8,24},{16,0},{24,8},{1,17},{9,25},{17,1},{25,9},{2,18},{10... | collective-permute-start | bytes 786440 | tf_op jit(solution)/shard_map/ppermute | solution.py:158
  89.2 1.9 %collective-permute-done.21.refs_4_ = bf16[256,512]{1,0:T(8,128)(2,1)S(1)} collective-permute-done((bf16[256,512]{1,0:T(8,128)(2,1)S(1)}, bf16[256,512]{1,0:T(8,128)(2,1)S(1)}, u32[]{:S(2)}, u32[]{:S(2)}) %collective-permute-start.21) | collective-permute-done | bytes 262176 | tf_op jit(solution)/shard_map/ppermute | solution.py:158
  97.9 5.4 %collective-permute-done.12.refs_4_ = bf16[256,512]{1,0:T(8,128)(2,1)S(1)} collective-permute-done((bf16[256,512]{1,0:T(8,128)(2,1)S(1)}, bf16[256,512]{1,0:T(8,128)(2,1)S(1)}, u32[]{:S(2)}, u32[]{:S(2)}) %collective-permute-start.12) | collective-permute-done | bytes 262176 | tf_op jit(solution)/shard_map/ppermute | solution.py:158
  105.7 5.8 %collective-permute-start.14 = (bf16[256,512]{1,0:T(8,128)(2,1)S(1)}, bf16[256,512]{1,0:T(8,128)(2,1)S(1)}, u32[]{:S(2)}, u32[]{:S(2)}) collective-permute-start(bf16[256,512]{1,0:T(8,128)(2,1)S(1)} %get-tuple-element.53), channel_id=1, source_target_pairs={{0,16},{8,24},{16,0},{24,8},{1,17},{9,25},{17,1},{25,9},{2,18},{10... | collective-permute-start | bytes 786440 | tf_op jit(solution)/shard_map/ppermute | solution.py:158
  114.5 3.6 %collective-permute-done.13.refs_1_ = bf16[256,512]{1,0:T(8,128)(2,1)S(1)} collective-permute-done((bf16[256,512]{1,0:T(8,128)(2,1)S(1)}, bf16[256,512]{1,0:T(8,128)(2,1)S(1)}, u32[]{:S(2)}, u32[]{:S(2)}) %collective-permute-start.13) | collective-permute-done | bytes 262176 | tf_op jit(solution)/shard_map/ppermute | solution.py:158
  118.0 2.1 %collective-permute-done.14.refs_2_ = bf16[256,512]{1,0:T(8,128)(2,1)S(1)} collective-permute-done((bf16[256,512]{1,0:T(8,128)(2,1)S(1)}, bf16[256,512]{1,0:T(8,128)(2,1)S(1)}, u32[]{:S(2)}, u32[]{:S(2)}) %collective-permute-start.14) | collective-permute-done | bytes 262176 | tf_op jit(solution)/shard_map/ppermute | solution.py:158
  120.1 4.6 %collective-permute-done.15.refs_3_ = bf16[256,512]{1,0:T(8,128)(2,1)S(1)} collective-permute-done((bf16[256,512]{1,0:T(8,128)(2,1)S(1)}, bf16[256,512]{1,0:T(8,128)(2,1)S(1)}, u32[]{:S(2)}, u32[]{:S(2)}) %collective-permute-start.15) | collective-permute-done | bytes 262176 | tf_op jit(solution)/shard_map/ppermute | solution.py:158
  132.5 10.4 %collective-permute-done.26.refs_0_ = bf16[256,1024]{1,0:T(8,128)(2,1)S(1)} collective-permute-done((bf16[256,1024]{1,0:T(8,128)(2,1)S(1)}, bf16[256,1024]{1,0:T(8,128)(2,1)S(1)}, u32[]{:S(2)}, u32[]{:S(2)}) %collective-permute-start.26) | collective-permute-done | bytes 524320 | tf_op jit(solution)/shard_map/ppermute | solution.py:158
  142.9 11.4 %collective-permute-done.27.refs_1_ = bf16[256,1024]{1,0:T(8,128)(2,1)S(1)} collective-permute-done((bf16[256,1024]{1,0:T(8,128)(2,1)S(1)}, bf16[256,1024]{1,0:T(8,128)(2,1)S(1)}, u32[]{:S(2)}, u32[]{:S(2)}) %collective-permute-start.27) | collective-permute-done | bytes 524320 | tf_op jit(solution)/shard_map/ppermute | solution.py:158
  (108 shorter events, 41.8 us)
Async XLA Ops:
  8.5 16.3 %all-to-all-start = ((bf16[2,4,4,32,256]{4,3,2,0,1:T(8,128)(2,1)}), bf16[2,4,4,32,256]{4,3,2,0,1:T(8,128)(2,1)}, u32[]{:S(2)}, u32[]{:S(2)}) async-start(bf16[2,4,4,32,256]{4,3,2,0,1:T(8,128)(2,1)} %copy.9), calls=%async_computation | async-start | bytes 1048576 | tf_op jit(solution)/shard_map/all_to_all | solution.py:186
  14.3 23.2 %collective-permute-start.1 = (bf16[4,4,32,256]{3,2,1,0:T(8,128)(2,1)S(1)}, bf16[4,4,32,256]{3,2,1,0:T(8,128)(2,1)S(1)}, u32[]{:S(2)}, u32[]{:S(2)}) collective-permute-start(bf16[4,4,32,256]{3,2,1,0:T(8,128)(2,1)S(1)} %slice_bitcast_fusion.2.refs_0_), channel_id=1, source_target_pairs={{0,2},{2,4},{4,6},{6,0},{1,3},{3,5},{5,7},{7,1},{8,10},{10,12},{12... | collective-permute-start | bytes 786440 | tf_op jit(solution)/shard_map/ppermute | solution.py:158
  17.6 19.8 %collective-permute-start.2 = (bf16[4,4,32,256]{3,2,1,0:T(8,128)(2,1)S(1)}, bf16[4,4,32,256]{3,2,1,0:T(8,128)(2,1)S(1)}, u32[]{:S(2)}, u32[]{:S(2)}) collective-permute-start(bf16[4,4,32,256]{3,2,1,0:T(8,128)(2,1)S(1)} %slice_bitcast_fusion.2.refs_0_), channel_id=1, source_target_pairs={{0,6},{2,0},{4,2},{6,4},{1,7},{3,1},{5,3},{7,5},{8,14},{10,8},{12,... | collective-permute-start | bytes 786440 | tf_op jit(solution)/shard_map/ppermute | solution.py:158
  19.8 26.4 %collective-permute-start.3 = (bf16[4,4,32,256]{3,2,1,0:T(8,128)(2,1)S(1)}, bf16[4,4,32,256]{3,2,1,0:T(8,128)(2,1)S(1)}, u32[]{:S(2)}, u32[]{:S(2)}) collective-permute-start(bf16[4,4,32,256]{3,2,1,0:T(8,128)(2,1)S(1)} %slice_bitcast_fusion.2.refs_0_), channel_id=1, source_target_pairs={{0,4},{2,6},{4,0},{6,2},{1,5},{3,7},{5,1},{7,3},{8,12},{10,14},{12... | collective-permute-start | bytes 786440 | tf_op jit(solution)/shard_map/ppermute | solution.py:158
  26.7 19.6 %all-to-all-start.1 = ((bf16[4,4,32,256]{3,2,1,0:T(8,128)(2,1)}), bf16[4,4,32,256]{3,2,1,0:T(8,128)(2,1)S(1)}, u32[]{:S(2)}, u32[]{:S(2)}) async-start(bf16[4,4,32,256]{3,2,1,0:T(8,128)(2,1)} %get-tuple-element.71), calls=%async_computation.1 | async-start | bytes 524288 | tf_op jit(solution)/shard_map/all_to_all | solution.py:187
  31.4 59.7 %all-gather.5.cloned.1.call-start = ((), (), s32[]{:S(2)}) async-start(), calls=%async_computation.3 | async-start | bytes 2359296 | tf_op jit(solution)/shard_map/all_gather | solution.py:191
  47.1 77.6 %all-gather.3.cloned.1.call-start = ((), (), s32[]{:S(2)}) async-start(), calls=%async_computation.2 | async-start | bytes 2359296 | tf_op jit(solution)/shard_map/all_gather | solution.py:191
  57.9 12.1 %collective-permute-start.17 = (bf16[256,512]{1,0:T(8,128)(2,1)}, bf16[256,512]{1,0:T(8,128)(2,1)S(1)}, u32[]{:S(2)}, u32[]{:S(2)}) collective-permute-start(bf16[256,512]{1,0:T(8,128)(2,1)} %get-tuple-element.57), channel_id=1, source_target_pairs={{0,64},{32,96},{64,0},{96,32},{1,65},{33,97},{65,1},{97,33},{2,66}... | collective-permute-start | bytes 786440 | tf_op jit(solution)/shard_map/ppermute | solution.py:158
  60.6 14.0 %collective-permute-start.18 = (bf16[256,512]{1,0:T(8,128)(2,1)}, bf16[256,512]{1,0:T(8,128)(2,1)S(1)}, u32[]{:S(2)}, u32[]{:S(2)}) collective-permute-start(bf16[256,512]{1,0:T(8,128)(2,1)} %get-tuple-element.58), channel_id=1, source_target_pairs={{0,96},{32,0},{64,32},{96,64},{1,97},{33,1},{65,33},{97,65},{2,98}... | collective-permute-start | bytes 786440 | tf_op jit(solution)/shard_map/ppermute | solution.py:158
  65.4 13.1 %collective-permute-start.7 = (bf16[256,512]{1,0:T(8,128)(2,1)}, bf16[256,512]{1,0:T(8,128)(2,1)S(1)}, u32[]{:S(2)}, u32[]{:S(2)}) collective-permute-start(bf16[256,512]{1,0:T(8,128)(2,1)} %get-tuple-element.44), channel_id=1, source_target_pairs={{0,32},{32,64},{64,96},{96,0},{1,33},{33,65},{65,97},{97,1},{2,34}... | collective-permute-start | bytes 786440 | tf_op jit(solution)/shard_map/ppermute | solution.py:158
  68.6 15.9 %collective-permute-start.9 = (bf16[256,512]{1,0:T(8,128)(2,1)}, bf16[256,512]{1,0:T(8,128)(2,1)S(1)}, u32[]{:S(2)}, u32[]{:S(2)}) collective-permute-start(bf16[256,512]{1,0:T(8,128)(2,1)} %get-tuple-element.46), channel_id=1, source_target_pairs={{0,96},{32,0},{64,32},{96,64},{1,97},{33,1},{65,33},{97,65},{2,98}... | collective-permute-start | bytes 786440 | tf_op jit(solution)/shard_map/ppermute | solution.py:158
  75.3 14.0 %collective-permute-start.19 = (bf16[256,512]{1,0:T(8,128)(2,1)S(1)}, bf16[256,512]{1,0:T(8,128)(2,1)S(1)}, u32[]{:S(2)}, u32[]{:S(2)}) collective-permute-start(bf16[256,512]{1,0:T(8,128)(2,1)S(1)} %get-tuple-element.60), channel_id=1, source_target_pairs={{0,8},{8,16},{16,24},{24,0},{1,9},{9,17},{17,25},{25,1},{2,10},{10... | collective-permute-start | bytes 786440 | tf_op jit(solution)/shard_map/ppermute | solution.py:158
  76.0 13.2 %collective-permute-start.20 = (bf16[256,512]{1,0:T(8,128)(2,1)S(1)}, bf16[256,512]{1,0:T(8,128)(2,1)S(1)}, u32[]{:S(2)}, u32[]{:S(2)}) collective-permute-start(bf16[256,512]{1,0:T(8,128)(2,1)S(1)} %get-tuple-element.61), channel_id=1, source_target_pairs={{0,16},{8,24},{16,0},{24,8},{1,17},{9,25},{17,1},{25,9},{2,18},{10... | collective-permute-start | bytes 786440 | tf_op jit(solution)/shard_map/ppermute | solution.py:158
  78.4 12.7 %collective-permute-start.21 = (bf16[256,512]{1,0:T(8,128)(2,1)S(1)}, bf16[256,512]{1,0:T(8,128)(2,1)S(1)}, u32[]{:S(2)}, u32[]{:S(2)}) collective-permute-start(bf16[256,512]{1,0:T(8,128)(2,1)S(1)} %get-tuple-element.62), channel_id=1, source_target_pairs={{0,24},{8,0},{16,8},{24,16},{1,25},{9,1},{17,9},{25,17},{2,26},{10... | collective-permute-start | bytes 786440 | tf_op jit(solution)/shard_map/ppermute | solution.py:158
  89.2 14.0 %collective-permute-start.12 = (bf16[256,512]{1,0:T(8,128)(2,1)S(1)}, bf16[256,512]{1,0:T(8,128)(2,1)S(1)}, u32[]{:S(2)}, u32[]{:S(2)}) collective-permute-start(bf16[256,512]{1,0:T(8,128)(2,1)S(1)} %get-tuple-element.50), channel_id=1, source_target_pairs={{0,24},{8,0},{16,8},{24,16},{1,25},{9,1},{17,9},{25,17},{2,26},{10... | collective-permute-start | bytes 786440 | tf_op jit(solution)/shard_map/ppermute | solution.py:158
  94.6 16.9 %collective-permute-start.22 = (bf16[256,512]{1,0:T(8,128)(2,1)S(1)}, bf16[256,512]{1,0:T(8,128)(2,1)S(1)}, u32[]{:S(2)}, u32[]{:S(2)}) collective-permute-start(bf16[256,512]{1,0:T(8,128)(2,1)S(1)} %get-tuple-element.64), channel_id=1, source_target_pairs={{0,8},{8,16},{16,24},{24,0},{1,9},{9,17},{17,25},{25,1},{2,10},{10... | collective-permute-start | bytes 786440 | tf_op jit(solution)/shard_map/ppermute | solution.py:158
  96.0 16.8 %collective-permute-start.23 = (bf16[256,512]{1,0:T(8,128)(2,1)S(1)}, bf16[256,512]{1,0:T(8,128)(2,1)S(1)}, u32[]{:S(2)}, u32[]{:S(2)}) collective-permute-start(bf16[256,512]{1,0:T(8,128)(2,1)S(1)} %get-tuple-element.65), channel_id=1, source_target_pairs={{0,16},{8,24},{16,0},{24,8},{1,17},{9,25},{17,1},{25,9},{2,18},{10... | collective-permute-start | bytes 786440 | tf_op jit(solution)/shard_map/ppermute | solution.py:158
  97.8 16.7 %collective-permute-start.24 = (bf16[256,512]{1,0:T(8,128)(2,1)S(1)}, bf16[256,512]{1,0:T(8,128)(2,1)S(1)}, u32[]{:S(2)}, u32[]{:S(2)}) collective-permute-start(bf16[256,512]{1,0:T(8,128)(2,1)S(1)} %get-tuple-element.66), channel_id=1, source_target_pairs={{0,24},{8,0},{16,8},{24,16},{1,25},{9,1},{17,9},{25,17},{2,26},{10... | collective-permute-start | bytes 786440 | tf_op jit(solution)/shard_map/ppermute | solution.py:158
  105.0 13.0 %collective-permute-start.13 = (bf16[256,512]{1,0:T(8,128)(2,1)S(1)}, bf16[256,512]{1,0:T(8,128)(2,1)S(1)}, u32[]{:S(2)}, u32[]{:S(2)}) collective-permute-start(bf16[256,512]{1,0:T(8,128)(2,1)S(1)} %get-tuple-element.52), channel_id=1, source_target_pairs={{0,8},{8,16},{16,24},{24,0},{1,9},{9,17},{17,25},{25,1},{2,10},{10... | collective-permute-start | bytes 786440 | tf_op jit(solution)/shard_map/ppermute | solution.py:158
  105.7 14.4 %collective-permute-start.14 = (bf16[256,512]{1,0:T(8,128)(2,1)S(1)}, bf16[256,512]{1,0:T(8,128)(2,1)S(1)}, u32[]{:S(2)}, u32[]{:S(2)}) collective-permute-start(bf16[256,512]{1,0:T(8,128)(2,1)S(1)} %get-tuple-element.53), channel_id=1, source_target_pairs={{0,16},{8,24},{16,0},{24,8},{1,17},{9,25},{17,1},{25,9},{2,18},{10... | collective-permute-start | bytes 786440 | tf_op jit(solution)/shard_map/ppermute | solution.py:158
  111.5 13.1 %collective-permute-start.15 = (bf16[256,512]{1,0:T(8,128)(2,1)S(1)}, bf16[256,512]{1,0:T(8,128)(2,1)S(1)}, u32[]{:S(2)}, u32[]{:S(2)}) collective-permute-start(bf16[256,512]{1,0:T(8,128)(2,1)S(1)} %get-tuple-element.54), channel_id=1, source_target_pairs={{0,24},{8,0},{16,8},{24,16},{1,25},{9,1},{17,9},{25,17},{2,26},{10... | collective-permute-start | bytes 786440 | tf_op jit(solution)/shard_map/ppermute | solution.py:158
  128.1 14.9 %collective-permute-start.26 = (bf16[256,1024]{1,0:T(8,128)(2,1)S(1)}, bf16[256,1024]{1,0:T(8,128)(2,1)S(1)}, u32[]{:S(2)}, u32[]{:S(2)}) collective-permute-start(bf16[256,1024]{1,0:T(8,128)(2,1)S(1)} %get-tuple-element.69), channel_id=1, source_target_pairs={{0,32},{32,64},{64,96},{96,0},{1,33},{33,65},{65,97},{97,1},{2,34}... | collective-permute-start | bytes 1572872 | tf_op jit(solution)/shard_map/ppermute | solution.py:158
  128.3 26.1 %collective-permute-start.27 = (bf16[256,1024]{1,0:T(8,128)(2,1)S(1)}, bf16[256,1024]{1,0:T(8,128)(2,1)S(1)}, u32[]{:S(2)}, u32[]{:S(2)}) collective-permute-start(bf16[256,1024]{1,0:T(8,128)(2,1)S(1)} %get-tuple-element.70), channel_id=1, source_target_pairs={{0,96},{32,0},{64,32},{96,64},{1,97},{33,1},{65,33},{97,65},{2,98}... | collective-permute-start | bytes 1572872 | tf_op jit(solution)/shard_map/ppermute | solution.py:158
  132.0 24.0 %collective-permute-start.25 = (bf16[256,1024]{1,0:T(8,128)(2,1)S(1)}, bf16[256,1024]{1,0:T(8,128)(2,1)S(1)}, u32[]{:S(2)}, u32[]{:S(2)}) collective-permute-start(bf16[256,1024]{1,0:T(8,128)(2,1)S(1)} %get-tuple-element.68), channel_id=1, source_target_pairs={{0,64},{32,96},{64,0},{96,32},{1,65},{33,97},{65,1},{97,33},{2,66}... | collective-permute-start | bytes 1572872 | tf_op jit(solution)/shard_map/ppermute | solution.py:158
  (30 other events, 257.5 us)
Sparse Core Ops, SparseCore 0:
  47.2 32.8 all-gather.4
  81.9 33.9 all-gather.2
